TPU v7x, 32 devices: a whole 2x2x4 slice. The times are simulated.
32 devices in a mesh: blk: 8 (over z, x), ulysses: 4 (over y, core).
Axes of the slice: x: 2, y: 2, z: 4, core: 2. Of those that a mesh axis runs over, the one named last changes fastest.
Arguments:
- tokens: bfloat16 [2, 2048, 768], P(None, ('blk', 'ulysses')), may hold values from -6 to 6
- attn_gain: bfloat16 [768], P(('blk', 'ulysses')), may hold values from 0.25 to 1.75
- qkv_weight: bfloat16 [768, 2304], P(('blk', 'ulysses')), may hold values from -0.3125 to 0.3125
- attn_out_weight: bfloat16 [768, 768], P(('blk', 'ulysses')), may hold values from -1.25 to 1.25
- mlp_gain: bfloat16 [768], P(('blk', 'ulysses')), may hold values from 0.25 to 1.75
- in_weight: bfloat16 [768, 2304], P(('blk', 'ulysses')), may hold values from -0.21875 to 0.21875
- out_weight: bfloat16 [1152, 768], P(None, ('blk', 'ulysses')), may hold values from -0.1875 to 0.1875
- cotangent: bfloat16 [2, 2048, 768], P(None, ('blk', 'ulysses')), may hold values from -6 to 6
Outputs:
- layer_output: bfloat16 [2, 2048, 768], P(None, ('blk', 'ulysses'))
- input_grad: bfloat16 [2, 2048, 768], P(None, ('blk', 'ulysses'))
- attn_gain_grad: float32 [768], P(('blk', 'ulysses'))
- qkv_weight_grad: float32 [768, 2304], P(('blk', 'ulysses'))
- attn_out_weight_grad: float32 [768, 768], P(('blk', 'ulysses'))
- mlp_gain_grad: float32 [768], P(('blk', 'ulysses'))
- in_weight_grad: float32 [768, 2304], P(('blk', 'ulysses'))
- out_weight_grad: float32 [1152, 768], P(None, ('blk', 'ulysses'))
All inputs are finite; a program needn't handle non-finite values.
Results may differ from a plain program's by a relative error of at most 0.018.
The roundings to bfloat16 on the way count: a program that leaves them out, or rounds other values in their place, can miss the bound.
Values may be sent and summed in bfloat16 or wider, within the bound.
No kernel may reach another device: no remote copies, remote signals or barrier semaphores. Data moves between devices by JAX's collectives and lax.ppermute only.
A program may use at most 256 MiB of HBM per device.

v0:
```python
import jax
import jax.numpy as jnp
from jax import lax
from jax.sharding import PartitionSpec as P

HEAD = 64
EPSILON = 1e-05
THETA = 160000.0


def from_behind(value, axis, by):
    size = lax.axis_size(axis)
    return lax.ppermute(value, axis, [(i, (i + by) % size) for i in range(size)])


def normalize(values):
    center = values - jnp.mean(values, axis=-1, keepdims=True)
    inverse = lax.rsqrt(jnp.mean(center * center, axis=-1, keepdims=True) + EPSILON)
    return (center * inverse, inverse)


def norm_back(grad_normed, normed, inverse):
    first_mean = jnp.mean(grad_normed, axis=-1, keepdims=True)
    second_mean = jnp.mean(grad_normed * normed, axis=-1, keepdims=True)
    return inverse * (grad_normed - first_mean - normed * second_mean)


def rotation(first_row, row_count, head_width):
    half_width = head_width // 2
    frequency = THETA ** (-(jnp.arange(half_width, dtype=jnp.float32) * 2.0) / head_width)
    positions = (first_row + jnp.arange(row_count, dtype=jnp.int32)).astype(jnp.float32)
    angles = positions[:, None] * frequency[None, :]
    cosine_table = jnp.concatenate([jnp.cos(angles), jnp.cos(angles)], axis=-1)
    sine_table = jnp.concatenate([jnp.sin(angles), jnp.sin(angles)], axis=-1)
    return (cosine_table, sine_table)


def rotate(values, cosine_table, sine_table, direction):
    half_width = values.shape[-1] // 2
    turned = jnp.concatenate([-values[..., half_width:], values[..., :half_width]], axis=-1)
    return values * cosine_table[:, None, :] + direction * turned * sine_table[:, None, :]


def block_grads(
    query_part,
    key_part,
    value_part,
    grad_part,
    log_part,
    dots_part,
    top_part,
    total_part,
    score_scale,
):
    scores = (
        jnp.einsum("sqhd,skhd->shqk", query_part, key_part, preferred_element_type=jnp.float32)
        * score_scale
    )
    probs = jnp.exp(scores - log_part[..., None])
    grad_probs = jnp.einsum(
        "sqhd,skhd->shqk", grad_part, value_part, preferred_element_type=jnp.float32
    )
    grad_scores = (probs * (grad_probs - dots_part[..., None])).astype(jnp.bfloat16)
    weights_low = jnp.exp(scores - top_part[..., None]).astype(jnp.bfloat16)
    grad_scaled = grad_part.astype(jnp.float32) / jnp.transpose(total_part, (0, 2, 1))[..., None]
    value_term = jnp.einsum("shqk,sqhd->skhd", weights_low.astype(jnp.float32), grad_scaled)
    return (value_term, grad_scores)


def body(
    tokens, attn_gain, qkv_weight, attn_out_weight, mlp_gain, in_weight, out_weight, cotangent
):
    sequences, per_device, model_width = tokens.shape
    groups = lax.axis_size("ulysses")
    cycle_size = lax.axis_size("blk")
    group_width = model_width // groups
    heads_here = group_width // HEAD
    group_rows = per_device * groups
    score_scale = HEAD ** (-0.5)
    qkv_full, attn_full, in_full, out_full, gain_one, gain_two = (
        lax.all_gather(qkv_weight, ("blk", "ulysses"), axis=0, tiled=True),
        lax.all_gather(attn_out_weight, ("blk", "ulysses"), axis=0, tiled=True),
        lax.all_gather(in_weight, ("blk", "ulysses"), axis=0, tiled=True),
        lax.all_gather(out_weight, ("blk", "ulysses"), axis=1, tiled=True),
        lax.all_gather(attn_gain, ("blk", "ulysses"), axis=0, tiled=True),
        lax.all_gather(mlp_gain, ("blk", "ulysses"), axis=0, tiled=True),
    )
    gain_one = gain_one.astype(jnp.float32)
    gain_two = gain_two.astype(jnp.float32)
    hidden_units = out_full.shape[0]
    inputs_wide = tokens.astype(jnp.float32).reshape(sequences * per_device, model_width)
    normed_one, inverse_one = normalize(inputs_wide)
    hidden_one = (normed_one * gain_one).astype(jnp.bfloat16)
    qkv = jnp.dot(hidden_one, qkv_full, preferred_element_type=jnp.float32).astype(jnp.bfloat16)
    packed = qkv.reshape(sequences, per_device, 3, groups, group_width)
    headwise = lax.all_to_all(packed, "ulysses", split_axis=3, concat_axis=1, tiled=True)
    headwise = headwise.reshape(sequences, group_rows, 3, heads_here, HEAD)
    cosine_table, sine_table = rotation(lax.axis_index("blk") * group_rows, group_rows, HEAD)
    queries = rotate(headwise[:, :, 0].astype(jnp.float32), cosine_table, sine_table, 1.0).astype(
        jnp.bfloat16
    )
    key_rows = rotate(headwise[:, :, 1].astype(jnp.float32), cosine_table, sine_table, 1.0).astype(
        jnp.bfloat16
    )
    value_rows = headwise[:, :, 2]
    start_top = jnp.full((sequences, heads_here, group_rows), -1e30, jnp.float32)
    zeros_rows = jnp.zeros((sequences, group_rows, heads_here, HEAD), jnp.float32)
    key_piece = lax.all_gather(key_rows, "blk", axis=1, tiled=True)
    value_piece = lax.all_gather(value_rows, "blk", axis=1, tiled=True)
    scores = (
        jnp.einsum("sqhd,skhd->shqk", queries, key_piece, preferred_element_type=jnp.float32)
        * score_scale
    )
    new_top = jnp.maximum(start_top, jnp.max(scores, axis=-1))
    weights = jnp.exp(scores - new_top[..., None])
    attend_row_total = jnp.sum(weights, axis=-1)
    update = jnp.einsum(
        "shqk,skhd->sqhd",
        weights.astype(jnp.bfloat16),
        value_piece,
        preferred_element_type=jnp.float32,
    )
    weighted = update
    row_top, row_total, weighted = (new_top, attend_row_total, weighted)
    log_total = row_top + jnp.log(row_total)
    attn_wide = weighted / jnp.transpose(row_total, (0, 2, 1))[..., None]
    attn_low = attn_wide.astype(jnp.bfloat16).reshape(sequences, group_rows, 1, group_width)
    token_rows = lax.all_to_all(attn_low, "ulysses", split_axis=1, concat_axis=2, tiled=True)
    attn_cat = token_rows.reshape(sequences * per_device, model_width)
    middle = inputs_wide + jnp.dot(attn_cat, attn_full, preferred_element_type=jnp.float32)
    normed_two, inverse_two = normalize(middle)
    hidden_two = (normed_two * gain_two).astype(jnp.bfloat16)
    joint = jnp.dot(hidden_two, in_full, preferred_element_type=jnp.float32)

    def geglu(joint_pre):
        return (
            jax.nn.gelu(joint_pre[:, :hidden_units], approximate=False)
            * joint_pre[:, hidden_units:]
        )

    act_wide, geglu_back = jax.vjp(geglu, joint)
    activation = act_wide.astype(jnp.bfloat16)
    result = middle + jnp.dot(activation, out_full, preferred_element_type=jnp.float32)
    layer_output = result.astype(jnp.bfloat16).reshape(sequences, per_device, model_width)
    grad_out = cotangent.reshape(sequences * per_device, model_width)
    grad_wout = jnp.einsum("tf,td->fd", activation, grad_out, preferred_element_type=jnp.float32)
    grad_act = jnp.einsum("td,fd->tf", grad_out, out_full, preferred_element_type=jnp.float32)
    grad_joint = geglu_back(grad_act)[0].astype(jnp.bfloat16)
    grad_win = jnp.einsum("tc,tf->cf", hidden_two, grad_joint, preferred_element_type=jnp.float32)
    grad_hidden_two = jnp.einsum(
        "tf,cf->tc", grad_joint, in_full, preferred_element_type=jnp.float32
    )
    grad_gain_two = jnp.sum(grad_hidden_two * normed_two, axis=0)
    grad_middle = grad_out.astype(jnp.float32) + norm_back(
        grad_hidden_two * gain_two, normed_two, inverse_two
    )
    grad_branch = grad_middle.astype(jnp.bfloat16)
    grad_wattn = jnp.einsum("tc,td->cd", attn_cat, grad_branch, preferred_element_type=jnp.float32)
    grad_cat = jnp.einsum(
        "td,cd->tc", grad_branch, attn_full, preferred_element_type=jnp.float32
    ).astype(jnp.bfloat16)
    grad_heads_in = lax.all_to_all(
        grad_cat.reshape(sequences, per_device, groups, group_width),
        "ulysses",
        split_axis=2,
        concat_axis=1,
        tiled=True,
    )
    grad_attn = grad_heads_in.reshape(sequences, group_rows, heads_here, HEAD)
    row_dots = jnp.transpose(jnp.sum(grad_attn.astype(jnp.float32) * attn_wide, axis=-1), (0, 2, 1))

    def cycle_step(step_index, state_now):
        key_now, value_now, grad_key, grad_value, grad_query = state_now
        value_term, grad_scores = block_grads(
            queries,
            key_now,
            value_now,
            grad_attn,
            log_total,
            row_dots,
            row_top,
            row_total,
            score_scale,
        )
        grad_value = grad_value + value_term
        grad_key = grad_key + score_scale * jnp.einsum(
            "shqk,sqhd->skhd", grad_scores, queries, preferred_element_type=jnp.float32
        )
        grad_query = grad_query + score_scale * jnp.einsum(
            "shqk,skhd->sqhd", grad_scores, key_now, preferred_element_type=jnp.float32
        )
        key_now, value_now = from_behind((key_now, value_now), "blk", 1)
        grad_key, grad_value = (
            from_behind(grad_key.astype(jnp.bfloat16), "blk", 1).astype(grad_key.dtype),
            from_behind(grad_value.astype(jnp.bfloat16), "blk", 1).astype(grad_value.dtype),
        )
        return (key_now, value_now, grad_key, grad_value, grad_query)

    final_state = lax.fori_loop(
        0, cycle_size, cycle_step, (key_rows, value_rows, zeros_rows, zeros_rows, zeros_rows)
    )
    grad_key, grad_value, grad_query = (final_state[2], final_state[3], final_state[4])
    grad_query = rotate(grad_query, cosine_table, sine_table, -1.0)
    grad_key = rotate(grad_key, cosine_table, sine_table, -1.0)
    grad_stack = jnp.stack([grad_query, grad_key, grad_value], axis=2).astype(jnp.bfloat16)
    grad_stack = grad_stack.reshape(sequences, group_rows, 3, 1, group_width)
    grad_tokens = lax.all_to_all(grad_stack, "ulysses", split_axis=1, concat_axis=3, tiled=True)
    grad_qkv = grad_tokens.reshape(sequences * per_device, 3 * model_width)
    grad_wqkv = jnp.einsum("tc,tf->cf", hidden_one, grad_qkv, preferred_element_type=jnp.float32)
    grad_hidden_one = jnp.einsum(
        "tf,cf->tc", grad_qkv, qkv_full, preferred_element_type=jnp.float32
    )
    grad_gain_one = jnp.sum(grad_hidden_one * normed_one, axis=0)
    grad_input = grad_middle + norm_back(grad_hidden_one * gain_one, normed_one, inverse_one)
    input_grad = grad_input.astype(jnp.bfloat16).reshape(sequences, per_device, model_width)
    shard_qkv, shard_attn, shard_in, shard_out, shard_one, shard_two = (
        lax.psum_scatter(grad_wqkv, ("blk", "ulysses"), scatter_dimension=0, tiled=True),
        lax.psum_scatter(grad_wattn, ("blk", "ulysses"), scatter_dimension=0, tiled=True),
        lax.psum_scatter(grad_win, ("blk", "ulysses"), scatter_dimension=0, tiled=True),
        lax.psum_scatter(grad_wout, ("blk", "ulysses"), scatter_dimension=1, tiled=True),
        lax.psum_scatter(grad_gain_one, ("blk", "ulysses"), scatter_dimension=0, tiled=True),
        lax.psum_scatter(grad_gain_two, ("blk", "ulysses"), scatter_dimension=0, tiled=True),
    )
    return (
        layer_output,
        input_grad,
        shard_one,
        shard_qkv,
        shard_attn,
        shard_two,
        shard_in,
        shard_out,
    )


def solution(mesh):
    placed = (
        P(None, ("blk", "ulysses"), None),
        P(("blk", "ulysses")),
        P(("blk", "ulysses"), None),
        P(("blk", "ulysses"), None),
        P(("blk", "ulysses")),
        P(("blk", "ulysses"), None),
        P(None, ("blk", "ulysses")),
        P(None, ("blk", "ulysses"), None),
    )
    return jax.shard_map(
        body,
        mesh=mesh,
        in_specs=placed,
        out_specs=(
            P(None, ("blk", "ulysses"), None),
            P(None, ("blk", "ulysses"), None),
            P(("blk", "ulysses")),
            P(("blk", "ulysses"), None),
            P(("blk", "ulysses"), None),
            P(("blk", "ulysses")),
            P(("blk", "ulysses"), None),
            P(None, ("blk", "ulysses")),
        ),
        check_vma=False,
    )
```

profile of v0, /device:TPU:0, one launch (start us, length us, event | category | flops | bytes accessed | tf_op | source)
XLA Modules:
  0.0 867.9 jit_solution(4147596167485549714)
XLA Ops:
  9.6 42.2 %all-reduce.8 = (bf16[768]{0:T(1024)(128)(2,1)S(1)}, bf16[768]{0:T(1024)(128)(2,1)S(1)}) all-reduce(bf16[768]{0:T(1024)(128)(2,1)S(1)} %dynamic-update-slice, bf16[768]{0:T(1024)(128)(2,1)S(1)} %dynamic-update-slice.1), channel_id=1, replica_groups=mesh['blk'=8,'ulysses'=4] {'blk','ulysses'}, use_global_device_ids=true, to_apply=%add.2 | all-reduce | flops 1536 | bytes 6144
  55.8 18.1 %all-gather.8.cloned.1.call-done = bf16[768,2304]{1,0:T(8,128)(2,1)} async-done(((bf16[24,2304]{1,0:T(8,128)(2,1)}), bf16[768,2304]{1,0:T(8,128)(2,1)}) %all-gather.8.cloned.1.call-update) | async-done | bytes 3538960 | tf_op jit(solution)/shard_map/all_gather | solution.py:81
  73.8 2.6 convolution_convert_fusion
  78.3 3.5 all-to-all-start
  82.7 10.7 %all-to-all-done = bf16[2,64,3,4,192]{4,1,2,0,3:T(8,128)(2,1)S(1)} async-done(((bf16[2,64,3,4,192]{4,1,2,0,3:T(8,128)(2,1)}), bf16[2,64,3,4,192]{4,1,2,0,3:T(8,128)(2,1)S(1)}, u32[]{:S(2)}, u32[]{:S(2)}) %all-to-all-start) | async-done | bytes 589856 | tf_op jit(solution)/shard_map/all_to_all | solution.py:96
  99.1 41.7 %all-gather.10.cloned.1.call-done = bf16[2,2048,3,64]{1,3,2,0:T(8,128)(2,1)} async-done(((bf16[2,256,3,64]{1,3,2,0:T(8,128)(2,1)}), bf16[2,2048,3,64]{1,3,2,0:T(8,128)(2,1)}) %all-gather.10.cloned.1.call-update) | async-done | bytes 1572880 | tf_op jit(solution)/shard_map/all_gather | solution.py:108
  140.8 3.3 multiply_reduce_fusion
  144.2 4.5 copy-done
  148.6 2.4 fusion.11
  151.1 35.8 %all-gather.18.cloned.1.call-done = bf16[2,2048,1,3,64]{1,4,3,0,2:T(8,128)(2,1)} async-done(((bf16[2,256,1,3,64]{1,4,3,0,2:T(8,128)(2,1)}), bf16[2,2048,1,3,64]{1,4,3,0,2:T(8,128)(2,1)}) %all-gather.18.cloned.1.call-update) | async-done | bytes 1572880 | tf_op jit(solution)/shard_map/all_gather | solution.py:109
  186.9 8.2 fusion.56
  196.0 3.4 all-to-all-start.1
  199.6 5.8 all-to-all-done.1
  205.9 36.1 %all-gather.12.cloned.1.call-done = bf16[768,768]{1,0:T(8,128)(2,1)} async-done(((bf16[24,768]{1,0:T(8,128)(2,1)}), bf16[768,768]{1,0:T(8,128)(2,1)}) %all-gather.12.cloned.1.call-update) | async-done | bytes 1179664 | tf_op jit(solution)/shard_map/all_gather | solution.py:82
  244.0 59.9 %all-gather.14.cloned.1.call-done = bf16[768,2304]{1,0:T(8,128)(2,1)} async-done(((bf16[24,2304]{1,0:T(8,128)(2,1)}), bf16[768,2304]{1,0:T(8,128)(2,1)}) %all-gather.14.cloned.1.call-update) | async-done | bytes 3538960 | tf_op jit(solution)/shard_map/all_gather | solution.py:83
  303.9 2.7 fusion.54
  306.6 54.5 %all-gather.16.cloned.1.call-done = bf16[1152,768]{0,1:T(8,128)(2,1)} async-done(((bf16[1152,24]{0,1:T(8,128)(2,1)}), bf16[1152,768]{0,1:T(8,128)(2,1)}) %all-gather.16.cloned.1.call-update) | async-done | bytes 1769488 | tf_op jit(solution)/shard_map/all_gather | solution.py:84
  361.1 3.2 fusion.45
  364.6 1.9 multiply_reduce_fusion.1
  366.8 1.9 fusion.46
  368.8 2.5 fusion.59
  375.7 3.4 all-to-all-start.2
  379.2 4.7 fusion.49
  387.3 184.9 %while.19 = (s32[]{:T(128)}, bf16[2,256,3,64]{1,3,2,0:T(8,128)(2,1)}, bf16[2,256,3,64]{1,3,2,0:T(8,128)(2,1)}, f32[2,256,3,64]{1,3,2,0:T(8,128)}, f32[2,256,3,64...) while((s32[]{:T(128)}, ...), condition=%wide.region_10.0_spmd.clone, body=%wide.region_9.0_spmd.clone.sunk | while | flops 255787008 | bytes 18751904 | solution.py:199
  395.6 2.0 fusion.110
  399.7 7.6 collective-permute-done.2
  407.3 1.7 convert_element_type.208
  416.4 2.0 fusion.110
  418.5 1.8 collective-permute-start.3
  420.3 2.1 fusion.111
  422.4 14.6 %collective-permute-done.2 = bf16[2,256,3,64]{1,3,2,0:T(8,128)(2,1)} collective-permute-done((bf16[2,256,3,64]{1,3,2,0:T(8,128)(2,1)}, bf16[2,256,3,64]{1,3,2,0:T(8,128)(2,1)}, u32[]{:S(2)}, u32[]{:S(2)}) %collective-permute-start.2) | collective-permute-done | bytes 196640 | tf_op jit(solution)/shard_map/while/body/eval_jaxpr/ppermute | solution.py:13
  437.0 1.7 convert_element_type.208
  444.8 2.0 fusion.110
  447.0 2.1 fusion.111
  449.1 12.9 %collective-permute-done.2 = bf16[2,256,3,64]{1,3,2,0:T(8,128)(2,1)} collective-permute-done((bf16[2,256,3,64]{1,3,2,0:T(8,128)(2,1)}, bf16[2,256,3,64]{1,3,2,0:T(8,128)(2,1)}, u32[]{:S(2)}, u32[]{:S(2)}) %collective-permute-start.2) | collective-permute-done | bytes 196640 | tf_op jit(solution)/shard_map/while/body/eval_jaxpr/ppermute | solution.py:13
  462.1 1.7 convert_element_type.208
  469.8 2.0 fusion.110
  471.9 2.2 fusion.111
  474.0 10.6 %collective-permute-done.2 = bf16[2,256,3,64]{1,3,2,0:T(8,128)(2,1)} collective-permute-done((bf16[2,256,3,64]{1,3,2,0:T(8,128)(2,1)}, bf16[2,256,3,64]{1,3,2,0:T(8,128)(2,1)}, u32[]{:S(2)}, u32[]{:S(2)}) %collective-permute-start.2) | collective-permute-done | bytes 196640 | tf_op jit(solution)/shard_map/while/body/eval_jaxpr/ppermute | solution.py:13
  492.4 2.0 fusion.110
  494.5 2.2 fusion.111
  496.6 8.0 collective-permute-done.2
  504.6 1.7 convert_element_type.208
  512.4 2.0 fusion.110
  514.4 2.9 collective-permute-start.3
  517.4 2.2 fusion.111
  519.6 4.2 collective-permute-done.2
  523.8 1.7 convert_element_type.208
  528.5 2.8 collective-permute-start.1
  534.4 2.0 fusion.110
  537.0 2.2 fusion.111
  539.1 3.9 collective-permute-done.2
  552.3 2.0 fusion.110
  554.4 1.9 collective-permute-start.3
  556.3 2.2 fusion.111
  558.5 11.0 %collective-permute-done.2 = bf16[2,256,3,64]{1,3,2,0:T(8,128)(2,1)} collective-permute-done((bf16[2,256,3,64]{1,3,2,0:T(8,128)(2,1)}, bf16[2,256,3,64]{1,3,2,0:T(8,128)(2,1)}, u32[]{:S(2)}, u32[]{:S(2)}) %collective-permute-start.2) | collective-permute-done | bytes 196640 | tf_op jit(solution)/shard_map/while/body/eval_jaxpr/ppermute | solution.py:13
  575.8 1.8 copy.48
  577.6 5.3 all-to-all-start.3
  583.1 11.5 %all-to-all-done.3 = bf16[2,256,3,1,192]{4,0,3,2,1:T(2,128)(2,1)S(1)} async-done(((bf16[2,256,3,1,192]{4,0,3,2,1:T(2,128)(2,1)}), bf16[2,256,3,1,192]{4,0,3,2,1:T(2,128)(2,1)S(1)}, u32[]{:S(2)}, u32[]{:S(2)}) %all-to-all-start.3) | async-done | bytes 589856 | tf_op jit(solution)/shard_map/all_to_all | solution.py:207
  596.0 4.0 fusion.58
  603.0 3.5 multiply_reduce_fusion.2
  606.4 37.0 %all-reduce.7 = (f32[768]{0:T(1024)S(1)}, f32[768]{0:T(1024)S(1)}) all-reduce(f32[768]{0:T(1024)S(1)} %get-tuple-element.116, f32[768]{0:T(1024)S(1)} %copy-done.28), channel_id=3, replica_groups=mesh['blk'=8,'ulysses'=4] {'blk','ulysses'}, use_global_device_ids=true, to_apply=%region_14.0.clone | all-reduce | flops 1536 | bytes 12288
  645.5 91.0 %reduce-scatter.11.cloned.1.call-done = f32[24,2304]{1,0:T(8,128)} async-done(((f32[768,2304]{1,0:T(8,128)}), f32[24,2304]{1,0:T(8,128)}) %reduce-scatter.11.cloned.1.call-update) | async-done | bytes 221200 | tf_op jit(solution)/shard_map/reduce_scatter | solution.py:219
  736.5 124.6 %reduce-scatter.7.cloned.1.call-done = f32[24,2304]{1,0:T(8,128)} async-done(((f32[768,2304]{1,0:T(8,128)}), f32[24,2304]{1,0:T(8,128)}) %reduce-scatter.7.cloned.1.call-update) | async-done | bytes 221200 | tf_op jit(solution)/shard_map/reduce_scatter | solution.py:217
  (321 shorter events, 98.6 us)
Async XLA Ops:
  7.2 66.7 %all-gather.8.cloned.1.call-start = ((), (), s32[]{:S(2)}) async-start(), calls=%async_computation.8 | async-start | bytes 3649536 | tf_op jit(solution)/shard_map/all_gather | solution.py:81
  51.8 22.0 %copy-start.21 = (f32[768]{0:T(1024)}, f32[768]{0:T(1024)S(1)}, u32[]{:S(2)}) copy-start(f32[768]{0:T(1024)S(1)} %convert_element_type.109) | copy-start | bytes 9220
  52.9 20.9 %copy-start.32 = (f32[128]{0:T(128)}, f32[128]{0:T(128)S(1)}, u32[]{:S(2)}) copy-start(f32[128]{0:T(128)S(1)} %div.49) | copy-start | bytes 1540
  54.2 19.7 %copy-start.34 = (f32[128]{0:T(128)}, f32[128]{0:T(128)S(1)}, u32[]{:S(2)}) copy-start(f32[128]{0:T(128)S(1)} %rsqrt.21) | copy-start | bytes 1540
  78.3 15.1 %all-to-all-start = ((bf16[2,64,3,4,192]{4,1,2,0,3:T(8,128)(2,1)}), bf16[2,64,3,4,192]{4,1,2,0,3:T(8,128)(2,1)S(1)}, u32[]{:S(2)}, u32[]{:S(2)}) async-start(bf16[2,64,3,4,192]{4,1,2,0,3:T(8,128)(2,1)} %copy.38), calls=%async_computation | async-start | bytes 1572864 | tf_op jit(solution)/shard_map/all_to_all | solution.py:96
  81.8 59.0 %all-gather.10.cloned.1.call-start = ((), (), s32[]{:S(2)}) async-start(), calls=%async_computation.9 | async-start | bytes 1769472 | tf_op jit(solution)/shard_map/all_gather | solution.py:108
  82.0 13.7 %copy-start.17 = (f32[256,64]{0,1:T(8,128)}, f32[256,64]{0,1:T(8,128)S(1)}, u32[]{:S(2)}) copy-start(f32[256,64]{0,1:T(8,128)S(1)} %pad_maximum_fusion.1) | copy-start | bytes 196612
  96.6 90.3 %all-gather.18.cloned.1.call-start = ((), (), s32[]{:S(2)}) async-start(), calls=%async_computation.16 | async-start | bytes 1769472 | tf_op jit(solution)/shard_map/all_gather | solution.py:109
  97.3 144.7 %all-gather.12.cloned.1.call-start = ((), (), s32[]{:S(2)}) async-start(), calls=%async_computation.10 | async-start | bytes 1216512 | tf_op jit(solution)/shard_map/all_gather | solution.py:82
  97.9 206.0 %all-gather.14.cloned.1.call-start = ((), (), s32[]{:S(2)}) async-start(), calls=%async_computation.11 | async-start | bytes 3649536 | tf_op jit(solution)/shard_map/all_gather | solution.py:83
  98.5 262.6 %all-gather.16.cloned.1.call-start = ((), (), s32[]{:S(2)}) async-start(), calls=%async_computation.12 | async-start | bytes 1824768 | tf_op jit(solution)/shard_map/all_gather | solution.py:84
  144.1 4.5 copy-start
  144.1 7.0 copy-start.27
  144.1 42.8 %copy-start.25 = (f32[2,3,256]{2,1,0:T(4,128)}, f32[2,3,256]{2,1,0:T(4,128)S(1)}, u32[]{:S(2)}) copy-start(f32[2,3,256]{2,1,0:T(4,128)S(1)} %broadcast_maximum_fusion) | copy-start | bytes 18436
  151.1 44.0 %copy-start.23 = (f32[2,3,256]{2,1,0:T(4,128)}, f32[2,3,256]{2,1,0:T(4,128)S(1)}, u32[]{:S(2)}) copy-start(f32[2,3,256]{2,1,0:T(4,128)S(1)} %fusion.11) | copy-start | bytes 18436
  195.1 46.9 %copy-start.5 = (bf16[2,64,768]{2,1,0:T(8,128)(2,1)S(1)}, bf16[2,64,768]{2,1,0:T(8,128)(2,1)}, u32[]{:S(2)}) copy-start(bf16[2,64,768]{2,1,0:T(8,128)(2,1)} %param.10) | copy-start | bytes 589828
  196.0 9.4 %all-to-all-start.1 = ((bf16[2,256,1,192]{3,0,2,1:T(2,128)(2,1)}), bf16[2,256,1,192]{3,0,2,1:T(2,128)(2,1)S(1)}, u32[]{:S(2)}, u32[]{:S(2)}) async-start(bf16[2,256,1,192]{3,0,2,1:T(2,128)(2,1)} %copy.43), calls=%async_computation.1 | async-start | bytes 524288 | tf_op jit(solution)/shard_map/all_to_all | solution.py:128
  199.4 446.1 %reduce-scatter.9.cloned.1.call-start = ((), (), s32[]{:S(2)}) async-start(), calls=%async_computation.14 | async-start | bytes 2433024 | tf_op jit(solution)/shard_map/reduce_scatter | solution.py:218
  243.9 122.6 %copy-start.29 = (f32[128]{0:T(128)}, f32[128]{0:T(128)S(1)}, u32[]{:S(2)}) copy-start(f32[128]{0:T(128)S(1)} %add_rsqrt_fusion.1) | copy-start | bytes 1540
  243.9 117.1 %copy-start.15 = (bf16[2,64,768]{2,1,0:T(8,128)(2,1)S(1)}, bf16[2,64,768]{2,1,0:T(8,128)(2,1)}, u32[]{:S(2)}) copy-start(bf16[2,64,768]{2,1,0:T(8,128)(2,1)} %param.17) | copy-start | bytes 589828
  364.6 4.2 copy-start.9
  366.8 5.4 copy-start.6
  368.7 276.7 %reduce-scatter.13.cloned.1.call-start = ((), (), s32[]{:S(2)}) async-start(), calls=%async_computation.17 | async-start | bytes 3649536
  371.3 7.9 copy-start.12
  375.7 9.4 %all-to-all-start.2 = ((bf16[2,64,4,192]{3,1,0,2:T(8,128)(2,1)}), bf16[2,64,4,192]{3,1,0,2:T(8,128)(2,1)S(1)}, u32[]{:S(2)}, u32[]{:S(2)}) async-start(bf16[2,64,4,192]{3,1,0,2:T(8,128)(2,1)} %copy.46), calls=%async_computation.2 | async-start | bytes 524288 | tf_op jit(solution)/shard_map/all_to_all | solution.py:162
  379.1 357.4 %reduce-scatter.11.cloned.1.call-start = ((), (), s32[]{:S(2)}) async-start(), calls=%async_computation.15 | async-start | bytes 7299072 | tf_op jit(solution)/shard_map/reduce_scatter | solution.py:219
  388.3 22.6 %collective-permute-start = (bf16[2,256,3,64]{1,3,2,0:T(8,128)(2,1)S(1)}, bf16[2,256,3,64]{1,3,2,0:T(8,128)(2,1)}, u32[]{:S(2)}, u32[]{:S(2)}) collective-permute-start(bf16[2,256,3,64]{1,3,2,0:T(8,128)(2,1)S(1)} %copy.62), channel_id=1, source_target_pairs={{0,4},{4,8},{8,12},{12,16},{16,20},{20,24},{24,28},{28,0},{1,5},{5... | collective-permute-start | bytes 589832 | tf_op jit(solution)/shard_map/while/body/eval_jaxpr/ppermute | solution.py:13
  390.6 20.3 %collective-permute-start.1 = (bf16[2,256,3,64]{1,3,2,0:T(8,128)(2,1)S(1)}, bf16[2,256,3,64]{1,3,2,0:T(8,128)(2,1)}, u32[]{:S(2)}, u32[]{:S(2)}) collective-permute-start(bf16[2,256,3,64]{1,3,2,0:T(8,128)(2,1)S(1)} %copy.63), channel_id=1, source_target_pairs={{0,4},{4,8},{8,12},{12,16},{16,20},{20,24},{24,28},{28,0},{1,5},{5... | collective-permute-start | bytes 589832 | tf_op jit(solution)/shard_map/while/body/eval_jaxpr/ppermute | solution.py:13
  394.2 13.1 %collective-permute-start.2 = (bf16[2,256,3,64]{1,3,2,0:T(8,128)(2,1)}, bf16[2,256,3,64]{1,3,2,0:T(8,128)(2,1)}, u32[]{:S(2)}, u32[]{:S(2)}) collective-permute-start(bf16[2,256,3,64]{1,3,2,0:T(8,128)(2,1)} %fusion.109), channel_id=1, source_target_pairs={{0,4},{4,8},{8,12},{12,16},{16,20},{20,24},{24,28},{28,0},{1,5},{5... | collective-permute-start | bytes 589832 | tf_op jit(solution)/shard_map/while/body/eval_jaxpr/ppermute | solution.py:13
  397.6 12.4 %collective-permute-start.3 = (bf16[2,256,3,64]{1,3,2,0:T(8,128)(2,1)}, bf16[2,256,3,64]{1,3,2,0:T(8,128)(2,1)S(1)}, u32[]{:S(2)}, u32[]{:S(2)}) collective-permute-start(bf16[2,256,3,64]{1,3,2,0:T(8,128)(2,1)} %fusion.110), channel_id=1, source_target_pairs={{0,4},{4,8},{8,12},{12,16},{16,20},{20,24},{24,28},{28,0},{1,5},{5... | collective-permute-start | bytes 589832 | tf_op jit(solution)/shard_map/while/body/eval_jaxpr/ppermute | solution.py:13
  411.8 28.1 %collective-permute-start = (bf16[2,256,3,64]{1,3,2,0:T(8,128)(2,1)S(1)}, bf16[2,256,3,64]{1,3,2,0:T(8,128)(2,1)}, u32[]{:S(2)}, u32[]{:S(2)}) collective-permute-start(bf16[2,256,3,64]{1,3,2,0:T(8,128)(2,1)S(1)} %copy.62), channel_id=1, source_target_pairs={{0,4},{4,8},{8,12},{12,16},{16,20},{20,24},{24,28},{28,0},{1,5},{5... | collective-permute-start | bytes 589832 | tf_op jit(solution)/shard_map/while/body/eval_jaxpr/ppermute | solution.py:13
  412.7 27.1 %collective-permute-start.1 = (bf16[2,256,3,64]{1,3,2,0:T(8,128)(2,1)S(1)}, bf16[2,256,3,64]{1,3,2,0:T(8,128)(2,1)}, u32[]{:S(2)}, u32[]{:S(2)}) collective-permute-start(bf16[2,256,3,64]{1,3,2,0:T(8,128)(2,1)S(1)} %copy.63), channel_id=1, source_target_pairs={{0,4},{4,8},{8,12},{12,16},{16,20},{20,24},{24,28},{28,0},{1,5},{5... | collective-permute-start | bytes 589832 | tf_op jit(solution)/shard_map/while/body/eval_jaxpr/ppermute | solution.py:13
  415.9 21.1 %collective-permute-start.2 = (bf16[2,256,3,64]{1,3,2,0:T(8,128)(2,1)}, bf16[2,256,3,64]{1,3,2,0:T(8,128)(2,1)}, u32[]{:S(2)}, u32[]{:S(2)}) collective-permute-start(bf16[2,256,3,64]{1,3,2,0:T(8,128)(2,1)} %fusion.109), channel_id=1, source_target_pairs={{0,4},{4,8},{8,12},{12,16},{16,20},{20,24},{24,28},{28,0},{1,5},{5... | collective-permute-start | bytes 589832 | tf_op jit(solution)/shard_map/while/body/eval_jaxpr/ppermute | solution.py:13
  418.5 20.6 %collective-permute-start.3 = (bf16[2,256,3,64]{1,3,2,0:T(8,128)(2,1)}, bf16[2,256,3,64]{1,3,2,0:T(8,128)(2,1)S(1)}, u32[]{:S(2)}, u32[]{:S(2)}) collective-permute-start(bf16[2,256,3,64]{1,3,2,0:T(8,128)(2,1)} %fusion.110), channel_id=1, source_target_pairs={{0,4},{4,8},{8,12},{12,16},{16,20},{20,24},{24,28},{28,0},{1,5},{5... | collective-permute-start | bytes 589832 | tf_op jit(solution)/shard_map/while/body/eval_jaxpr/ppermute | solution.py:13
  440.8 24.1 %collective-permute-start = (bf16[2,256,3,64]{1,3,2,0:T(8,128)(2,1)S(1)}, bf16[2,256,3,64]{1,3,2,0:T(8,128)(2,1)}, u32[]{:S(2)}, u32[]{:S(2)}) collective-permute-start(bf16[2,256,3,64]{1,3,2,0:T(8,128)(2,1)S(1)} %copy.62), channel_id=1, source_target_pairs={{0,4},{4,8},{8,12},{12,16},{16,20},{20,24},{24,28},{28,0},{1,5},{5... | collective-permute-start | bytes 589832 | tf_op jit(solution)/shard_map/while/body/eval_jaxpr/ppermute | solution.py:13
  441.7 23.2 %collective-permute-start.1 = (bf16[2,256,3,64]{1,3,2,0:T(8,128)(2,1)S(1)}, bf16[2,256,3,64]{1,3,2,0:T(8,128)(2,1)}, u32[]{:S(2)}, u32[]{:S(2)}) collective-permute-start(bf16[2,256,3,64]{1,3,2,0:T(8,128)(2,1)S(1)} %copy.63), channel_id=1, source_target_pairs={{0,4},{4,8},{8,12},{12,16},{16,20},{20,24},{24,28},{28,0},{1,5},{5... | collective-permute-start | bytes 589832 | tf_op jit(solution)/shard_map/while/body/eval_jaxpr/ppermute | solution.py:13
  444.8 17.3 %collective-permute-start.2 = (bf16[2,256,3,64]{1,3,2,0:T(8,128)(2,1)}, bf16[2,256,3,64]{1,3,2,0:T(8,128)(2,1)}, u32[]{:S(2)}, u32[]{:S(2)}) collective-permute-start(bf16[2,256,3,64]{1,3,2,0:T(8,128)(2,1)} %fusion.109), channel_id=1, source_target_pairs={{0,4},{4,8},{8,12},{12,16},{16,20},{20,24},{24,28},{28,0},{1,5},{5... | collective-permute-start | bytes 589832 | tf_op jit(solution)/shard_map/while/body/eval_jaxpr/ppermute | solution.py:13
  446.8 17.2 %collective-permute-start.3 = (bf16[2,256,3,64]{1,3,2,0:T(8,128)(2,1)}, bf16[2,256,3,64]{1,3,2,0:T(8,128)(2,1)S(1)}, u32[]{:S(2)}, u32[]{:S(2)}) collective-permute-start(bf16[2,256,3,64]{1,3,2,0:T(8,128)(2,1)} %fusion.110), channel_id=1, source_target_pairs={{0,4},{4,8},{8,12},{12,16},{16,20},{20,24},{24,28},{28,0},{1,5},{5... | collective-permute-start | bytes 589832 | tf_op jit(solution)/shard_map/while/body/eval_jaxpr/ppermute | solution.py:13
  465.8 21.6 %collective-permute-start = (bf16[2,256,3,64]{1,3,2,0:T(8,128)(2,1)S(1)}, bf16[2,256,3,64]{1,3,2,0:T(8,128)(2,1)}, u32[]{:S(2)}, u32[]{:S(2)}) collective-permute-start(bf16[2,256,3,64]{1,3,2,0:T(8,128)(2,1)S(1)} %copy.62), channel_id=1, source_target_pairs={{0,4},{4,8},{8,12},{12,16},{16,20},{20,24},{24,28},{28,0},{1,5},{5... | collective-permute-start | bytes 589832 | tf_op jit(solution)/shard_map/while/body/eval_jaxpr/ppermute | solution.py:13
  466.7 20.7 %collective-permute-start.1 = (bf16[2,256,3,64]{1,3,2,0:T(8,128)(2,1)S(1)}, bf16[2,256,3,64]{1,3,2,0:T(8,128)(2,1)}, u32[]{:S(2)}, u32[]{:S(2)}) collective-permute-start(bf16[2,256,3,64]{1,3,2,0:T(8,128)(2,1)S(1)} %copy.63), channel_id=1, source_target_pairs={{0,4},{4,8},{8,12},{12,16},{16,20},{20,24},{24,28},{28,0},{1,5},{5... | collective-permute-start | bytes 589832 | tf_op jit(solution)/shard_map/while/body/eval_jaxpr/ppermute | solution.py:13
  469.8 14.8 %collective-permute-start.2 = (bf16[2,256,3,64]{1,3,2,0:T(8,128)(2,1)}, bf16[2,256,3,64]{1,3,2,0:T(8,128)(2,1)}, u32[]{:S(2)}, u32[]{:S(2)}) collective-permute-start(bf16[2,256,3,64]{1,3,2,0:T(8,128)(2,1)} %fusion.109), channel_id=1, source_target_pairs={{0,4},{4,8},{8,12},{12,16},{16,20},{20,24},{24,28},{28,0},{1,5},{5... | collective-permute-start | bytes 589832 | tf_op jit(solution)/shard_map/while/body/eval_jaxpr/ppermute | solution.py:13
  471.9 14.8 %collective-permute-start.3 = (bf16[2,256,3,64]{1,3,2,0:T(8,128)(2,1)}, bf16[2,256,3,64]{1,3,2,0:T(8,128)(2,1)S(1)}, u32[]{:S(2)}, u32[]{:S(2)}) collective-permute-start(bf16[2,256,3,64]{1,3,2,0:T(8,128)(2,1)} %fusion.110), channel_id=1, source_target_pairs={{0,4},{4,8},{8,12},{12,16},{16,20},{20,24},{24,28},{28,0},{1,5},{5... | collective-permute-start | bytes 589832 | tf_op jit(solution)/shard_map/while/body/eval_jaxpr/ppermute | solution.py:13
  488.4 19.0 %collective-permute-start = (bf16[2,256,3,64]{1,3,2,0:T(8,128)(2,1)S(1)}, bf16[2,256,3,64]{1,3,2,0:T(8,128)(2,1)}, u32[]{:S(2)}, u32[]{:S(2)}) collective-permute-start(bf16[2,256,3,64]{1,3,2,0:T(8,128)(2,1)S(1)} %copy.62), channel_id=1, source_target_pairs={{0,4},{4,8},{8,12},{12,16},{16,20},{20,24},{24,28},{28,0},{1,5},{5... | collective-permute-start | bytes 589832 | tf_op jit(solution)/shard_map/while/body/eval_jaxpr/ppermute | solution.py:13
  489.3 18.1 %collective-permute-start.1 = (bf16[2,256,3,64]{1,3,2,0:T(8,128)(2,1)S(1)}, bf16[2,256,3,64]{1,3,2,0:T(8,128)(2,1)}, u32[]{:S(2)}, u32[]{:S(2)}) collective-permute-start(bf16[2,256,3,64]{1,3,2,0:T(8,128)(2,1)S(1)} %copy.63), channel_id=1, source_target_pairs={{0,4},{4,8},{8,12},{12,16},{16,20},{20,24},{24,28},{28,0},{1,5},{5... | collective-permute-start | bytes 589832 | tf_op jit(solution)/shard_map/while/body/eval_jaxpr/ppermute | solution.py:13
  492.4 12.2 %collective-permute-start.2 = (bf16[2,256,3,64]{1,3,2,0:T(8,128)(2,1)}, bf16[2,256,3,64]{1,3,2,0:T(8,128)(2,1)}, u32[]{:S(2)}, u32[]{:S(2)}) collective-permute-start(bf16[2,256,3,64]{1,3,2,0:T(8,128)(2,1)} %fusion.109), channel_id=1, source_target_pairs={{0,4},{4,8},{8,12},{12,16},{16,20},{20,24},{24,28},{28,0},{1,5},{5... | collective-permute-start | bytes 589832 | tf_op jit(solution)/shard_map/while/body/eval_jaxpr/ppermute | solution.py:13
  494.5 12.2 %collective-permute-start.3 = (bf16[2,256,3,64]{1,3,2,0:T(8,128)(2,1)}, bf16[2,256,3,64]{1,3,2,0:T(8,128)(2,1)S(1)}, u32[]{:S(2)}, u32[]{:S(2)}) collective-permute-start(bf16[2,256,3,64]{1,3,2,0:T(8,128)(2,1)} %fusion.110), channel_id=1, source_target_pairs={{0,4},{4,8},{8,12},{12,16},{16,20},{20,24},{24,28},{28,0},{1,5},{5... | collective-permute-start | bytes 589832 | tf_op jit(solution)/shard_map/while/body/eval_jaxpr/ppermute | solution.py:13
  508.4 18.2 %collective-permute-start = (bf16[2,256,3,64]{1,3,2,0:T(8,128)(2,1)S(1)}, bf16[2,256,3,64]{1,3,2,0:T(8,128)(2,1)}, u32[]{:S(2)}, u32[]{:S(2)}) collective-permute-start(bf16[2,256,3,64]{1,3,2,0:T(8,128)(2,1)S(1)} %copy.62), channel_id=1, source_target_pairs={{0,4},{4,8},{8,12},{12,16},{16,20},{20,24},{24,28},{28,0},{1,5},{5... | collective-permute-start | bytes 589832 | tf_op jit(solution)/shard_map/while/body/eval_jaxpr/ppermute | solution.py:13
  509.3 17.3 %collective-permute-start.1 = (bf16[2,256,3,64]{1,3,2,0:T(8,128)(2,1)S(1)}, bf16[2,256,3,64]{1,3,2,0:T(8,128)(2,1)}, u32[]{:S(2)}, u32[]{:S(2)}) collective-permute-start(bf16[2,256,3,64]{1,3,2,0:T(8,128)(2,1)S(1)} %copy.63), channel_id=1, source_target_pairs={{0,4},{4,8},{8,12},{12,16},{16,20},{20,24},{24,28},{28,0},{1,5},{5... | collective-permute-start | bytes 589832 | tf_op jit(solution)/shard_map/while/body/eval_jaxpr/ppermute | solution.py:13
  512.4 11.4 %collective-permute-start.2 = (bf16[2,256,3,64]{1,3,2,0:T(8,128)(2,1)}, bf16[2,256,3,64]{1,3,2,0:T(8,128)(2,1)}, u32[]{:S(2)}, u32[]{:S(2)}) collective-permute-start(bf16[2,256,3,64]{1,3,2,0:T(8,128)(2,1)} %fusion.109), channel_id=1, source_target_pairs={{0,4},{4,8},{8,12},{12,16},{16,20},{20,24},{24,28},{28,0},{1,5},{5... | collective-permute-start | bytes 589832 | tf_op jit(solution)/shard_map/while/body/eval_jaxpr/ppermute | solution.py:13
  514.4 11.3 %collective-permute-start.3 = (bf16[2,256,3,64]{1,3,2,0:T(8,128)(2,1)}, bf16[2,256,3,64]{1,3,2,0:T(8,128)(2,1)S(1)}, u32[]{:S(2)}, u32[]{:S(2)}) collective-permute-start(bf16[2,256,3,64]{1,3,2,0:T(8,128)(2,1)} %fusion.110), channel_id=1, source_target_pairs={{0,4},{4,8},{8,12},{12,16},{16,20},{20,24},{24,28},{28,0},{1,5},{5... | collective-permute-start | bytes 589832 | tf_op jit(solution)/shard_map/while/body/eval_jaxpr/ppermute | solution.py:13
  527.6 18.5 %collective-permute-start = (bf16[2,256,3,64]{1,3,2,0:T(8,128)(2,1)S(1)}, bf16[2,256,3,64]{1,3,2,0:T(8,128)(2,1)}, u32[]{:S(2)}, u32[]{:S(2)}) collective-permute-start(bf16[2,256,3,64]{1,3,2,0:T(8,128)(2,1)S(1)} %copy.62), channel_id=1, source_target_pairs={{0,4},{4,8},{8,12},{12,16},{16,20},{20,24},{24,28},{28,0},{1,5},{5... | collective-permute-start | bytes 589832 | tf_op jit(solution)/shard_map/while/body/eval_jaxpr/ppermute | solution.py:13
  528.5 17.6 %collective-permute-start.1 = (bf16[2,256,3,64]{1,3,2,0:T(8,128)(2,1)S(1)}, bf16[2,256,3,64]{1,3,2,0:T(8,128)(2,1)}, u32[]{:S(2)}, u32[]{:S(2)}) collective-permute-start(bf16[2,256,3,64]{1,3,2,0:T(8,128)(2,1)S(1)} %copy.63), channel_id=1, source_target_pairs={{0,4},{4,8},{8,12},{12,16},{16,20},{20,24},{24,28},{28,0},{1,5},{5... | collective-permute-start | bytes 589832 | tf_op jit(solution)/shard_map/while/body/eval_jaxpr/ppermute | solution.py:13
  534.4 8.7 %collective-permute-start.2 = (bf16[2,256,3,64]{1,3,2,0:T(8,128)(2,1)}, bf16[2,256,3,64]{1,3,2,0:T(8,128)(2,1)}, u32[]{:S(2)}, u32[]{:S(2)}) collective-permute-start(bf16[2,256,3,64]{1,3,2,0:T(8,128)(2,1)} %fusion.109), channel_id=1, source_target_pairs={{0,4},{4,8},{8,12},{12,16},{16,20},{20,24},{24,28},{28,0},{1,5},{5... | collective-permute-start | bytes 589832 | tf_op jit(solution)/shard_map/while/body/eval_jaxpr/ppermute | solution.py:13
  536.4 8.8 %collective-permute-start.3 = (bf16[2,256,3,64]{1,3,2,0:T(8,128)(2,1)}, bf16[2,256,3,64]{1,3,2,0:T(8,128)(2,1)S(1)}, u32[]{:S(2)}, u32[]{:S(2)}) collective-permute-start(bf16[2,256,3,64]{1,3,2,0:T(8,128)(2,1)} %fusion.110), channel_id=1, source_target_pairs={{0,4},{4,8},{8,12},{12,16},{16,20},{20,24},{24,28},{28,0},{1,5},{5... | collective-permute-start | bytes 589832 | tf_op jit(solution)/shard_map/while/body/eval_jaxpr/ppermute | solution.py:13
  547.0 25.2 %collective-permute-start = (bf16[2,256,3,64]{1,3,2,0:T(8,128)(2,1)S(1)}, bf16[2,256,3,64]{1,3,2,0:T(8,128)(2,1)}, u32[]{:S(2)}, u32[]{:S(2)}) collective-permute-start(bf16[2,256,3,64]{1,3,2,0:T(8,128)(2,1)S(1)} %copy.62), channel_id=1, source_target_pairs={{0,4},{4,8},{8,12},{12,16},{16,20},{20,24},{24,28},{28,0},{1,5},{5... | collective-permute-start | bytes 589832 | tf_op jit(solution)/shard_map/while/body/eval_jaxpr/ppermute | solution.py:13
  547.9 24.3 %collective-permute-start.1 = (bf16[2,256,3,64]{1,3,2,0:T(8,128)(2,1)S(1)}, bf16[2,256,3,64]{1,3,2,0:T(8,128)(2,1)}, u32[]{:S(2)}, u32[]{:S(2)}) collective-permute-start(bf16[2,256,3,64]{1,3,2,0:T(8,128)(2,1)S(1)} %copy.63), channel_id=1, source_target_pairs={{0,4},{4,8},{8,12},{12,16},{16,20},{20,24},{24,28},{28,0},{1,5},{5... | collective-permute-start | bytes 589832 | tf_op jit(solution)/shard_map/while/body/eval_jaxpr/ppermute | solution.py:13
  551.8 17.6 %collective-permute-start.2 = (bf16[2,256,3,64]{1,3,2,0:T(8,128)(2,1)}, bf16[2,256,3,64]{1,3,2,0:T(8,128)(2,1)}, u32[]{:S(2)}, u32[]{:S(2)}) collective-permute-start(bf16[2,256,3,64]{1,3,2,0:T(8,128)(2,1)} %fusion.109), channel_id=1, source_target_pairs={{0,4},{4,8},{8,12},{12,16},{16,20},{20,24},{24,28},{28,0},{1,5},{5... | collective-permute-start | bytes 589832 | tf_op jit(solution)/shard_map/while/body/eval_jaxpr/ppermute | solution.py:13
  554.4 17.0 %collective-permute-start.3 = (bf16[2,256,3,64]{1,3,2,0:T(8,128)(2,1)}, bf16[2,256,3,64]{1,3,2,0:T(8,128)(2,1)S(1)}, u32[]{:S(2)}, u32[]{:S(2)}) collective-permute-start(bf16[2,256,3,64]{1,3,2,0:T(8,128)(2,1)} %fusion.110), channel_id=1, source_target_pairs={{0,4},{4,8},{8,12},{12,16},{16,20},{20,24},{24,28},{28,0},{1,5},{5... | collective-permute-start | bytes 589832 | tf_op jit(solution)/shard_map/while/body/eval_jaxpr/ppermute | solution.py:13
  575.7 7.2 copy-start.22
  575.7 7.2 copy-start.31
  575.7 7.2 copy-start.37
  577.6 16.9 %all-to-all-start.3 = ((bf16[2,256,3,1,192]{4,0,3,2,1:T(2,128)(2,1)}), bf16[2,256,3,1,192]{4,0,3,2,1:T(2,128)(2,1)S(1)}, u32[]{:S(2)}, u32[]{:S(2)}) async-start(bf16[2,256,3,1,192]{4,0,3,2,1:T(2,128)(2,1)} %copy.48), calls=%async_computation.3 | async-start | bytes 1572864 | tf_op jit(solution)/shard_map/all_to_all | solution.py:207
  582.9 278.1 %reduce-scatter.7.cloned.1.call-start = ((), (), s32[]{:S(2)}) async-start(), calls=%async_computation.13 | async-start | bytes 7299072 | tf_op jit(solution)/shard_map/reduce_scatter | solution.py:217
  602.9 41.6 %copy-start.7 = (f32[128,768]{1,0:T(8,128)S(1)}, f32[128,768]{1,0:T(8,128)}, u32[]{:S(2)}) copy-start(f32[128,768]{1,0:T(8,128)} %copy-done.6) | copy-start | bytes 1179652
  (48 other events, 122.1 us)
Sparse Core Ops, SparseCore 0:
  10.9 62.8 all-gather.7
  96.7 44.0 all-gather.9
  143.4 43.4 all-gather.17
  189.7 52.2 all-gather.11
  244.8 59.0 all-gather.13
  306.6 54.4 all-gather.15
  368.8 114.1 reduce-scatter.8
  489.9 121.3 reduce-scatter.12
  618.6 117.8 reduce-scatter.10
  742.6 118.4 reduce-scatter.6
where the time goes:
time: 870 us; the launch traced here: 868 us
  waiting for transfers between devices  570 us (66%)
  matrix products  99.2 us (11%)
  blocking collectives  79.2 us (9%)
  local copies, waits for them, and re-layouts  36 us (4%)
  other arithmetic  35.4 us (4%)
  starting transfers between devices  32.5 us (4%)
  between operations  14.8 us (2%)
    reduce_scatter x1, waiting for transfers between devices, body(): lax.psum_scatter(grad_wqkv, ('blk', 'ulysses'), scatter_dimension=0, tile...  125 us
    reduce_scatter x1, waiting for transfers between devices, body(): lax.psum_scatter(grad_win, ('blk', 'ulysses'), scatter_dimension=0, tiled...  91 us
    unnamed x2, blocking collectives  79.2 us
    ppermute x32, waiting for transfers between devices, from_behind(): lax.ppermute(value, axis, [(i, (i + by) % size) for i in range(size)])  76.3 us
    all_gather x1, waiting for transfers between devices, body(): lax.all_gather(in_weight, ('blk', 'ulysses'), axis=0, tiled=True)  59.9 us
    all_gather x1, waiting for transfers between devices, body(): lax.all_gather(out_weight, ('blk', 'ulysses'), axis=1, tiled=True)  54.5 us
    all_gather x1, waiting for transfers between devices, body(): key_piece = lax.all_gather(key_rows, 'blk', axis=1, tiled=True)  41.7 us
    all_gather x1, waiting for transfers between devices, body(): lax.all_gather(attn_out_weight, ('blk', 'ulysses'), axis=0, tiled=True)  36.1 us
  transfers between devices with their start and end apart: 46, of which 28 were waited for; matrix products, arithmetic and copies ran while one was open for 17% of the time, Pallas kernels for 0%

commit v1 on v0

--- a/solution.py
+++ b/solution.py
@@ -6,6 +6,27 @@
 HEAD = 64
 EPSILON = 1e-05
 THETA = 160000.0
+
+
+def in_order(blocks, dim):
+    shape = list(blocks.shape[1:])
+    shape[dim] *= blocks.shape[0]
+    return jnp.moveaxis(blocks, 0, dim).reshape(shape)
+
+
+def grow_blocks(array, axis):
+    size, index = (lax.axis_size(axis), lax.axis_index(axis))
+    tiles, distance = (array[None], 1)
+    while distance < size:
+        other = lax.ppermute(tiles, axis, [(i, i ^ distance) for i in range(size)])
+        low = index & distance == 0
+        tiles = jnp.concatenate([jnp.where(low, tiles, other), jnp.where(low, other, tiles)])
+        distance *= 2
+    return tiles
+
+
+def gather_by_bits(array, axis, dim):
+    return in_order(grow_blocks(array, axis), dim)
 
 
 def from_behind(value, axis, by):
@@ -106,7 +127,7 @@
     start_top = jnp.full((sequences, heads_here, group_rows), -1e30, jnp.float32)
     zeros_rows = jnp.zeros((sequences, group_rows, heads_here, HEAD), jnp.float32)
     key_piece = lax.all_gather(key_rows, "blk", axis=1, tiled=True)
-    value_piece = lax.all_gather(value_rows, "blk", axis=1, tiled=True)
+    value_piece = gather_by_bits(value_rows, "blk", 1)
     scores = (
         jnp.einsum("sqhd,skhd->shqk", queries, key_piece, preferred_element_type=jnp.float32)
         * score_scale

time: 870 us -> 844 us (0.970)
  waiting for transfers between devices: 570 us -> 549 us
    ppermute x0 -> x3, waiting for transfers between devices: none -> 67.2 us  [grow_blocks(): other = lax.ppermute(tiles, axis, [(i, i ^ distance) for i in range(size)])]
    all_gather x1, waiting for transfers between devices: 41.7 us -> 0.02 us  [body(): key_piece = lax.all_gather(key_rows, 'blk', axis=1, tiled=True)]
    all_gather x1 -> x0, waiting for transfers between devices: 35.8 us -> none  [body(): value_piece = lax.all_gather(value_rows, 'blk', axis=1, tiled=True)]
    all_gather x1, waiting for transfers between devices: 36.1 us -> 25.9 us  [body(): lax.all_gather(attn_out_weight, ('blk', 'ulysses'), axis=0, tiled=True)]
  transfers between devices with their start and end apart: 46 -> 48, of which waited for: 28 -> 29; matrix products, arithmetic and copies ran while one was open for 17% -> 17% of each run, Pallas kernels for 0% -> 0%
where the time goes in v1:
time: 844 us; the launch traced here: 842 us
  waiting for transfers between devices  549 us (65%)
  matrix products  94.3 us (11%)
  blocking collectives  79.2 us (9%)
  starting transfers between devices  36.3 us (4%)
  other arithmetic  36.1 us (4%)
  local copies, waits for them, and re-layouts  32.3 us (4%)
  between operations  14.5 us (2%)
    reduce_scatter x1, waiting for transfers between devices, body(): lax.psum_scatter(grad_wqkv, ('blk', 'ulysses'), scatter_dimension=0, tile...  125 us
    reduce_scatter x1, waiting for transfers between devices, body(): lax.psum_scatter(grad_win, ('blk', 'ulysses'), scatter_dimension=0, tiled...  91.2 us
    unnamed x2, blocking collectives  79.2 us
    ppermute x32, waiting for transfers between devices, from_behind(): lax.ppermute(value, axis, [(i, (i + by) % size) for i in range(size)])  75.8 us
    ppermute x3, waiting for transfers between devices, grow_blocks(): other = lax.ppermute(tiles, axis, [(i, i ^ distance) for i in range(size)])  67.2 us
    all_gather x1, waiting for transfers between devices, body(): lax.all_gather(in_weight, ('blk', 'ulysses'), axis=0, tiled=True)  59.9 us
    all_gather x1, waiting for transfers between devices, body(): lax.all_gather(out_weight, ('blk', 'ulysses'), axis=1, tiled=True)  54.5 us
    all_gather x1, waiting for transfers between devices, body(): lax.all_gather(attn_out_weight, ('blk', 'ulysses'), axis=0, tiled=True)  25.9 us
  transfers between devices with their start and end apart: 48, of which 29 were waited for; matrix products, arithmetic and copies ran while one was open for 17% of the time, Pallas kernels for 0%

profile of v1, /device:TPU:0, one launch (start us, length us, event | category | flops | bytes accessed | tf_op | source)
XLA Modules:
  0.0 842.0 jit_solution(14238017529634290865)
XLA Ops:
  9.6 42.2 %all-reduce.8 = (bf16[768]{0:T(1024)(128)(2,1)S(1)}, bf16[768]{0:T(1024)(128)(2,1)S(1)}) all-reduce(bf16[768]{0:T(1024)(128)(2,1)S(1)} %dynamic-update-slice, bf16[768]{0:T(1024)(128)(2,1)S(1)} %dynamic-update-slice.1), channel_id=1, replica_groups=mesh['blk'=8,'ulysses'=4] {'blk','ulysses'}, use_global_device_ids=true, to_apply=%add.2 | all-reduce | flops 1536 | bytes 6144
  55.8 18.1 %all-gather.6.cloned.1.call-done = bf16[768,2304]{1,0:T(8,128)(2,1)} async-done(((bf16[24,2304]{1,0:T(8,128)(2,1)}), bf16[768,2304]{1,0:T(8,128)(2,1)}) %all-gather.6.cloned.1.call-update) | async-done | bytes 3538960 | tf_op jit(solution)/shard_map/all_gather | solution.py:102
  73.8 2.6 convolution_convert_fusion
  78.3 3.5 all-to-all-start
  82.7 10.7 %all-to-all-done = bf16[2,64,3,4,192]{4,1,2,0,3:T(8,128)(2,1)S(1)} async-done(((bf16[2,64,3,4,192]{4,1,2,0,3:T(8,128)(2,1)}), bf16[2,64,3,4,192]{4,1,2,0,3:T(8,128)(2,1)S(1)}, u32[]{:S(2)}, u32[]{:S(2)}) %all-to-all-start) | async-done | bytes 589856 | tf_op jit(solution)/shard_map/all_to_all | solution.py:117
  99.4 5.0 collective-permute-done.4
  105.5 15.1 %collective-permute-done.5 = bf16[2,2,256,3,64]{2,4,3,1,0:T(8,128)(2,1)S(1)} collective-permute-done((bf16[2,2,256,3,64]{2,4,3,1,0:T(8,128)(2,1)S(1)}, bf16[2,2,256,3,64]{2,4,3,1,0:T(8,128)(2,1)S(1)}, u32[]{:S(2)}, u32[]{:S(2)}) %collective-permute-start.5) | collective-permute-done | bytes 393248 | tf_op jit(solution)/shard_map/ppermute | solution.py:21
  122.0 47.0 %collective-permute-done.6 = bf16[4,2,256,3,64]{2,4,3,1,0:T(8,128)(2,1)S(1)} collective-permute-done((bf16[4,2,256,3,64]{2,4,3,1,0:T(8,128)(2,1)S(1)}, bf16[4,2,256,3,64]{2,4,3,1,0:T(8,128)(2,1)S(1)}, u32[]{:S(2)}, u32[]{:S(2)}) %collective-permute-start.6) | collective-permute-done | bytes 786464 | tf_op jit(solution)/shard_map/ppermute | solution.py:21
  169.5 3.3 multiply_reduce_fusion
  173.4 2.4 fusion.11
  175.9 3.2 fusion.51
  180.0 3.4 all-to-all-start.1
  183.7 6.3 all-to-all-done.1
  190.4 25.9 %all-gather.10.cloned.1.call-done = bf16[768,768]{1,0:T(8,128)(2,1)} async-done(((bf16[24,768]{1,0:T(8,128)(2,1)}), bf16[768,768]{1,0:T(8,128)(2,1)}) %all-gather.10.cloned.1.call-update) | async-done | bytes 1179664 | tf_op jit(solution)/shard_map/all_gather | solution.py:103
  218.2 59.9 %all-gather.12.cloned.1.call-done = bf16[768,2304]{1,0:T(8,128)(2,1)} async-done(((bf16[24,2304]{1,0:T(8,128)(2,1)}), bf16[768,2304]{1,0:T(8,128)(2,1)}) %all-gather.12.cloned.1.call-update) | async-done | bytes 3538960 | tf_op jit(solution)/shard_map/all_gather | solution.py:104
  278.2 2.7 fusion.49
  280.9 54.5 %all-gather.14.cloned.1.call-done = bf16[1152,768]{0,1:T(8,128)(2,1)} async-done(((bf16[1152,24]{0,1:T(8,128)(2,1)}), bf16[1152,768]{0,1:T(8,128)(2,1)}) %all-gather.14.cloned.1.call-update) | async-done | bytes 1769488 | tf_op jit(solution)/shard_map/all_gather | solution.py:105
  335.3 3.2 fusion.40
  338.9 1.9 multiply_reduce_fusion.1
  341.1 1.9 fusion.41
  343.1 2.5 fusion.54
  350.0 3.4 all-to-all-start.2
  353.4 4.7 fusion.44
  361.6 184.7 %while.19 = (s32[]{:T(128)}, bf16[2,256,3,64]{1,3,2,0:T(8,128)(2,1)}, bf16[2,256,3,64]{1,3,2,0:T(8,128)(2,1)}, f32[2,256,3,64]{1,3,2,0:T(8,128)}, f32[2,256,3,64...) while((s32[]{:T(128)}, ...), condition=%wide.region_10.11_spmd.clone, body=%wide.region_9.10_spmd.clone.sunk | while | flops 255787008 | bytes 18751904 | solution.py:220
  369.8 2.0 fusion.106
  374.0 7.6 collective-permute-done.2
  381.6 1.8 convert_element_type.208
  390.7 2.0 fusion.106
  392.7 1.8 collective-permute-start.3
  394.5 2.2 fusion.107
  396.7 14.6 %collective-permute-done.2 = bf16[2,256,3,64]{1,3,2,0:T(8,128)(2,1)} collective-permute-done((bf16[2,256,3,64]{1,3,2,0:T(8,128)(2,1)}, bf16[2,256,3,64]{1,3,2,0:T(8,128)(2,1)}, u32[]{:S(2)}, u32[]{:S(2)}) %collective-permute-start.2) | collective-permute-done | bytes 196640 | tf_op jit(solution)/shard_map/while/body/eval_jaxpr/ppermute | solution.py:34
  411.3 1.8 convert_element_type.208
  419.0 2.0 fusion.106
  421.2 2.2 fusion.107
  423.3 12.9 %collective-permute-done.2 = bf16[2,256,3,64]{1,3,2,0:T(8,128)(2,1)} collective-permute-done((bf16[2,256,3,64]{1,3,2,0:T(8,128)(2,1)}, bf16[2,256,3,64]{1,3,2,0:T(8,128)(2,1)}, u32[]{:S(2)}, u32[]{:S(2)}) %collective-permute-start.2) | collective-permute-done | bytes 196640 | tf_op jit(solution)/shard_map/while/body/eval_jaxpr/ppermute | solution.py:34
  444.0 2.0 fusion.106
  446.0 2.2 fusion.107
  448.2 10.6 %collective-permute-done.2 = bf16[2,256,3,64]{1,3,2,0:T(8,128)(2,1)} collective-permute-done((bf16[2,256,3,64]{1,3,2,0:T(8,128)(2,1)}, bf16[2,256,3,64]{1,3,2,0:T(8,128)(2,1)}, u32[]{:S(2)}, u32[]{:S(2)}) %collective-permute-start.2) | collective-permute-done | bytes 196640 | tf_op jit(solution)/shard_map/while/body/eval_jaxpr/ppermute | solution.py:34
  466.5 2.0 fusion.106
  468.5 2.2 fusion.107
  470.7 8.0 collective-permute-done.2
  478.7 1.8 convert_element_type.208
  486.4 2.0 fusion.106
  488.5 3.0 collective-permute-start.3
  491.4 2.2 fusion.107
  493.6 4.3 collective-permute-done.2
  497.9 1.8 convert_element_type.208
  502.6 2.8 collective-permute-start.1
  508.4 2.0 fusion.106
  511.0 2.2 fusion.107
  513.1 4.0 collective-permute-done.2
  517.1 1.8 convert_element_type.208
  526.3 2.0 fusion.106
  528.4 1.9 collective-permute-start.3
  530.2 2.2 fusion.107
  532.4 11.1 %collective-permute-done.2 = bf16[2,256,3,64]{1,3,2,0:T(8,128)(2,1)} collective-permute-done((bf16[2,256,3,64]{1,3,2,0:T(8,128)(2,1)}, bf16[2,256,3,64]{1,3,2,0:T(8,128)(2,1)}, u32[]{:S(2)}, u32[]{:S(2)}) %collective-permute-start.2) | collective-permute-done | bytes 196640 | tf_op jit(solution)/shard_map/while/body/eval_jaxpr/ppermute | solution.py:34
  549.8 1.9 copy.48
  551.7 5.4 all-to-all-start.3
  557.3 11.5 %all-to-all-done.3 = bf16[2,256,3,1,192]{4,0,3,2,1:T(2,128)(2,1)S(1)} async-done(((bf16[2,256,3,1,192]{4,0,3,2,1:T(2,128)(2,1)}), bf16[2,256,3,1,192]{4,0,3,2,1:T(2,128)(2,1)S(1)}, u32[]{:S(2)}, u32[]{:S(2)}) %all-to-all-start.3) | async-done | bytes 589856 | tf_op jit(solution)/shard_map/all_to_all | solution.py:228
  570.2 4.0 fusion.53
  577.1 3.5 multiply_reduce_fusion.2
  580.6 37.0 %all-reduce.7 = (f32[768]{0:T(1024)S(1)}, f32[768]{0:T(1024)S(1)}) all-reduce(f32[768]{0:T(1024)S(1)} %get-tuple-element.116, f32[768]{0:T(1024)S(1)} %copy-done.27), channel_id=2, replica_groups=mesh['blk'=8,'ulysses'=4] {'blk','ulysses'}, use_global_device_ids=true, to_apply=%region_14.15.clone | all-reduce | flops 1536 | bytes 12288
  619.6 91.2 %reduce-scatter.11.cloned.1.call-done = f32[24,2304]{1,0:T(8,128)} async-done(((f32[768,2304]{1,0:T(8,128)}), f32[24,2304]{1,0:T(8,128)}) %reduce-scatter.11.cloned.1.call-update) | async-done | bytes 221200 | tf_op jit(solution)/shard_map/reduce_scatter | solution.py:240
  710.9 124.7 %reduce-scatter.7.cloned.1.call-done = f32[24,2304]{1,0:T(8,128)} async-done(((f32[768,2304]{1,0:T(8,128)}), f32[24,2304]{1,0:T(8,128)}) %reduce-scatter.7.cloned.1.call-update) | async-done | bytes 221200 | tf_op jit(solution)/shard_map/reduce_scatter | solution.py:238
  (329 shorter events, 101.8 us)
Async XLA Ops:
  7.2 66.7 %all-gather.6.cloned.1.call-start = ((), (), s32[]{:S(2)}) async-start(), calls=%async_computation.8 | async-start | bytes 3649536 | tf_op jit(solution)/shard_map/all_gather | solution.py:102
  51.8 22.0 %copy-start.20 = (f32[768]{0:T(1024)}, f32[768]{0:T(1024)S(1)}, u32[]{:S(2)}) copy-start(f32[768]{0:T(1024)S(1)} %convert_element_type.109) | copy-start | bytes 9220
  52.9 20.9 %copy-start.31 = (f32[128]{0:T(128)}, f32[128]{0:T(128)S(1)}, u32[]{:S(2)}) copy-start(f32[128]{0:T(128)S(1)} %div.49) | copy-start | bytes 1540
  54.2 19.7 %copy-start.33 = (f32[128]{0:T(128)}, f32[128]{0:T(128)S(1)}, u32[]{:S(2)}) copy-start(f32[128]{0:T(128)S(1)} %rsqrt.21) | copy-start | bytes 1540
  78.3 15.1 %all-to-all-start = ((bf16[2,64,3,4,192]{4,1,2,0,3:T(8,128)(2,1)}), bf16[2,64,3,4,192]{4,1,2,0,3:T(8,128)(2,1)S(1)}, u32[]{:S(2)}, u32[]{:S(2)}) async-start(bf16[2,64,3,4,192]{4,1,2,0,3:T(8,128)(2,1)} %copy.38), calls=%async_computation | async-start | bytes 1572864 | tf_op jit(solution)/shard_map/all_to_all | solution.py:117
  81.8 87.7 %all-gather.8.cloned.1.call-start = ((), (), s32[]{:S(2)}) async-start(), calls=%async_computation.9 | async-start | bytes 1769472 | tf_op jit(solution)/shard_map/all_gather | solution.py:129
  82.0 13.7 %copy-start.16 = (f32[256,64]{0,1:T(8,128)}, f32[256,64]{0,1:T(8,128)S(1)}, u32[]{:S(2)}) copy-start(f32[256,64]{0,1:T(8,128)S(1)} %pad_maximum_fusion.3) | copy-start | bytes 196612
  96.5 119.8 %all-gather.10.cloned.1.call-start = ((), (), s32[]{:S(2)}) async-start(), calls=%async_computation.10 | async-start | bytes 1216512 | tf_op jit(solution)/shard_map/all_gather | solution.py:103
  97.3 180.9 %all-gather.12.cloned.1.call-start = ((), (), s32[]{:S(2)}) async-start(), calls=%async_computation.11 | async-start | bytes 3649536 | tf_op jit(solution)/shard_map/all_gather | solution.py:104
  97.8 237.5 %all-gather.14.cloned.1.call-start = ((), (), s32[]{:S(2)}) async-start(), calls=%async_computation.12 | async-start | bytes 1824768 | tf_op jit(solution)/shard_map/all_gather | solution.py:105
  97.9 6.5 collective-permute-start.4
  104.5 16.1 %collective-permute-start.5 = (bf16[2,2,256,3,64]{2,4,3,1,0:T(8,128)(2,1)S(1)}, bf16[2,2,256,3,64]{2,4,3,1,0:T(8,128)(2,1)S(1)}, u32[]{:S(2)}, u32[]{:S(2)}) collective-permute-start(bf16[2,2,256,3,64]{2,4,3,1,0:T(8,128)(2,1)S(1)} %pad_maximum_fusion.2), channel_id=1, source_target_pairs={{0,8},{4,12},{8,0},{12,4},{16,24},{20,28},{24,16},{28,20},{1,9},{5... | collective-permute-start | bytes 1179656 | tf_op jit(solution)/shard_map/ppermute | solution.py:21
  120.8 48.2 %collective-permute-start.6 = (bf16[4,2,256,3,64]{2,4,3,1,0:T(8,128)(2,1)S(1)}, bf16[4,2,256,3,64]{2,4,3,1,0:T(8,128)(2,1)S(1)}, u32[]{:S(2)}, u32[]{:S(2)}) collective-permute-start(bf16[4,2,256,3,64]{2,4,3,1,0:T(8,128)(2,1)S(1)} %pad_maximum_fusion), channel_id=1, source_target_pairs={{0,16},{4,20},{8,24},{12,28},{16,0},{20,4},{24,8},{28,12},{1,17},{... | collective-permute-start | bytes 2359304 | tf_op jit(solution)/shard_map/ppermute | solution.py:21
  179.1 37.2 %copy-start.4 = (bf16[2,64,768]{2,1,0:T(8,128)(2,1)S(1)}, bf16[2,64,768]{2,1,0:T(8,128)(2,1)}, u32[]{:S(2)}) copy-start(bf16[2,64,768]{2,1,0:T(8,128)(2,1)} %param.10) | copy-start | bytes 589828
  180.0 9.9 %all-to-all-start.1 = ((bf16[2,256,1,192]{3,0,2,1:T(2,128)(2,1)}), bf16[2,256,1,192]{3,0,2,1:T(2,128)(2,1)S(1)}, u32[]{:S(2)}, u32[]{:S(2)}) async-start(bf16[2,256,1,192]{3,0,2,1:T(2,128)(2,1)} %copy.43), calls=%async_computation.1 | async-start | bytes 524288 | tf_op jit(solution)/shard_map/all_to_all | solution.py:149
  183.4 436.2 %reduce-scatter.9.cloned.1.call-start = ((), (), s32[]{:S(2)}) async-start(), calls=%async_computation.14 | async-start | bytes 2433024 | tf_op jit(solution)/shard_map/reduce_scatter | solution.py:239
  218.2 122.6 %copy-start.28 = (f32[128]{0:T(128)}, f32[128]{0:T(128)S(1)}, u32[]{:S(2)}) copy-start(f32[128]{0:T(128)S(1)} %add_rsqrt_fusion.1) | copy-start | bytes 1540
  218.2 117.1 %copy-start.14 = (bf16[2,64,768]{2,1,0:T(8,128)(2,1)S(1)}, bf16[2,64,768]{2,1,0:T(8,128)(2,1)}, u32[]{:S(2)}) copy-start(bf16[2,64,768]{2,1,0:T(8,128)(2,1)} %param.17) | copy-start | bytes 589828
  338.9 4.2 copy-start.8
  341.0 5.4 copy-start.5
  343.0 276.6 %reduce-scatter.13.cloned.1.call-start = ((), (), s32[]{:S(2)}) async-start(), calls=%async_computation.16 | async-start | bytes 3649536
  345.5 7.9 copy-start.11
  350.0 9.4 %all-to-all-start.2 = ((bf16[2,64,4,192]{3,1,0,2:T(8,128)(2,1)}), bf16[2,64,4,192]{3,1,0,2:T(8,128)(2,1)S(1)}, u32[]{:S(2)}, u32[]{:S(2)}) async-start(bf16[2,64,4,192]{3,1,0,2:T(8,128)(2,1)} %copy.46), calls=%async_computation.2 | async-start | bytes 524288 | tf_op jit(solution)/shard_map/all_to_all | solution.py:183
  353.4 357.5 %reduce-scatter.11.cloned.1.call-start = ((), (), s32[]{:S(2)}) async-start(), calls=%async_computation.15 | async-start | bytes 7299072 | tf_op jit(solution)/shard_map/reduce_scatter | solution.py:240
  362.5 22.6 %collective-permute-start = (bf16[2,256,3,64]{1,3,2,0:T(8,128)(2,1)S(1)}, bf16[2,256,3,64]{1,3,2,0:T(8,128)(2,1)}, u32[]{:S(2)}, u32[]{:S(2)}) collective-permute-start(bf16[2,256,3,64]{1,3,2,0:T(8,128)(2,1)S(1)} %copy.63), channel_id=1, source_target_pairs={{0,4},{4,8},{8,12},{12,16},{16,20},{20,24},{24,28},{28,0},{1,5},{5... | collective-permute-start | bytes 589832 | tf_op jit(solution)/shard_map/while/body/eval_jaxpr/ppermute | solution.py:34
  364.9 20.2 %collective-permute-start.1 = (bf16[2,256,3,64]{1,3,2,0:T(8,128)(2,1)S(1)}, bf16[2,256,3,64]{1,3,2,0:T(8,128)(2,1)}, u32[]{:S(2)}, u32[]{:S(2)}) collective-permute-start(bf16[2,256,3,64]{1,3,2,0:T(8,128)(2,1)S(1)} %copy.64), channel_id=1, source_target_pairs={{0,4},{4,8},{8,12},{12,16},{16,20},{20,24},{24,28},{28,0},{1,5},{5... | collective-permute-start | bytes 589832 | tf_op jit(solution)/shard_map/while/body/eval_jaxpr/ppermute | solution.py:34
  365.8 4.0 copy-start.18
  365.9 4.0 copy-start.23
  368.5 13.1 %collective-permute-start.2 = (bf16[2,256,3,64]{1,3,2,0:T(8,128)(2,1)}, bf16[2,256,3,64]{1,3,2,0:T(8,128)(2,1)}, u32[]{:S(2)}, u32[]{:S(2)}) collective-permute-start(bf16[2,256,3,64]{1,3,2,0:T(8,128)(2,1)} %fusion.105), channel_id=1, source_target_pairs={{0,4},{4,8},{8,12},{12,16},{16,20},{20,24},{24,28},{28,0},{1,5},{5... | collective-permute-start | bytes 589832 | tf_op jit(solution)/shard_map/while/body/eval_jaxpr/ppermute | solution.py:34
  371.9 12.4 %collective-permute-start.3 = (bf16[2,256,3,64]{1,3,2,0:T(8,128)(2,1)}, bf16[2,256,3,64]{1,3,2,0:T(8,128)(2,1)S(1)}, u32[]{:S(2)}, u32[]{:S(2)}) collective-permute-start(bf16[2,256,3,64]{1,3,2,0:T(8,128)(2,1)} %fusion.106), channel_id=1, source_target_pairs={{0,4},{4,8},{8,12},{12,16},{16,20},{20,24},{24,28},{28,0},{1,5},{5... | collective-permute-start | bytes 589832 | tf_op jit(solution)/shard_map/while/body/eval_jaxpr/ppermute | solution.py:34
  386.0 28.0 %collective-permute-start = (bf16[2,256,3,64]{1,3,2,0:T(8,128)(2,1)S(1)}, bf16[2,256,3,64]{1,3,2,0:T(8,128)(2,1)}, u32[]{:S(2)}, u32[]{:S(2)}) collective-permute-start(bf16[2,256,3,64]{1,3,2,0:T(8,128)(2,1)S(1)} %copy.63), channel_id=1, source_target_pairs={{0,4},{4,8},{8,12},{12,16},{16,20},{20,24},{24,28},{28,0},{1,5},{5... | collective-permute-start | bytes 589832 | tf_op jit(solution)/shard_map/while/body/eval_jaxpr/ppermute | solution.py:34
  387.0 27.1 %collective-permute-start.1 = (bf16[2,256,3,64]{1,3,2,0:T(8,128)(2,1)S(1)}, bf16[2,256,3,64]{1,3,2,0:T(8,128)(2,1)}, u32[]{:S(2)}, u32[]{:S(2)}) collective-permute-start(bf16[2,256,3,64]{1,3,2,0:T(8,128)(2,1)S(1)} %copy.64), channel_id=1, source_target_pairs={{0,4},{4,8},{8,12},{12,16},{16,20},{20,24},{24,28},{28,0},{1,5},{5... | collective-permute-start | bytes 589832 | tf_op jit(solution)/shard_map/while/body/eval_jaxpr/ppermute | solution.py:34
  390.2 21.1 %collective-permute-start.2 = (bf16[2,256,3,64]{1,3,2,0:T(8,128)(2,1)}, bf16[2,256,3,64]{1,3,2,0:T(8,128)(2,1)}, u32[]{:S(2)}, u32[]{:S(2)}) collective-permute-start(bf16[2,256,3,64]{1,3,2,0:T(8,128)(2,1)} %fusion.105), channel_id=1, source_target_pairs={{0,4},{4,8},{8,12},{12,16},{16,20},{20,24},{24,28},{28,0},{1,5},{5... | collective-permute-start | bytes 589832 | tf_op jit(solution)/shard_map/while/body/eval_jaxpr/ppermute | solution.py:34
  392.7 20.6 %collective-permute-start.3 = (bf16[2,256,3,64]{1,3,2,0:T(8,128)(2,1)}, bf16[2,256,3,64]{1,3,2,0:T(8,128)(2,1)S(1)}, u32[]{:S(2)}, u32[]{:S(2)}) collective-permute-start(bf16[2,256,3,64]{1,3,2,0:T(8,128)(2,1)} %fusion.106), channel_id=1, source_target_pairs={{0,4},{4,8},{8,12},{12,16},{16,20},{20,24},{24,28},{28,0},{1,5},{5... | collective-permute-start | bytes 589832 | tf_op jit(solution)/shard_map/while/body/eval_jaxpr/ppermute | solution.py:34
  415.0 24.0 %collective-permute-start = (bf16[2,256,3,64]{1,3,2,0:T(8,128)(2,1)S(1)}, bf16[2,256,3,64]{1,3,2,0:T(8,128)(2,1)}, u32[]{:S(2)}, u32[]{:S(2)}) collective-permute-start(bf16[2,256,3,64]{1,3,2,0:T(8,128)(2,1)S(1)} %copy.63), channel_id=1, source_target_pairs={{0,4},{4,8},{8,12},{12,16},{16,20},{20,24},{24,28},{28,0},{1,5},{5... | collective-permute-start | bytes 589832 | tf_op jit(solution)/shard_map/while/body/eval_jaxpr/ppermute | solution.py:34
  415.9 23.1 %collective-permute-start.1 = (bf16[2,256,3,64]{1,3,2,0:T(8,128)(2,1)S(1)}, bf16[2,256,3,64]{1,3,2,0:T(8,128)(2,1)}, u32[]{:S(2)}, u32[]{:S(2)}) collective-permute-start(bf16[2,256,3,64]{1,3,2,0:T(8,128)(2,1)S(1)} %copy.64), channel_id=1, source_target_pairs={{0,4},{4,8},{8,12},{12,16},{16,20},{20,24},{24,28},{28,0},{1,5},{5... | collective-permute-start | bytes 589832 | tf_op jit(solution)/shard_map/while/body/eval_jaxpr/ppermute | solution.py:34
  419.0 17.2 %collective-permute-start.2 = (bf16[2,256,3,64]{1,3,2,0:T(8,128)(2,1)}, bf16[2,256,3,64]{1,3,2,0:T(8,128)(2,1)}, u32[]{:S(2)}, u32[]{:S(2)}) collective-permute-start(bf16[2,256,3,64]{1,3,2,0:T(8,128)(2,1)} %fusion.105), channel_id=1, source_target_pairs={{0,4},{4,8},{8,12},{12,16},{16,20},{20,24},{24,28},{28,0},{1,5},{5... | collective-permute-start | bytes 589832 | tf_op jit(solution)/shard_map/while/body/eval_jaxpr/ppermute | solution.py:34
  421.0 17.2 %collective-permute-start.3 = (bf16[2,256,3,64]{1,3,2,0:T(8,128)(2,1)}, bf16[2,256,3,64]{1,3,2,0:T(8,128)(2,1)S(1)}, u32[]{:S(2)}, u32[]{:S(2)}) collective-permute-start(bf16[2,256,3,64]{1,3,2,0:T(8,128)(2,1)} %fusion.106), channel_id=1, source_target_pairs={{0,4},{4,8},{8,12},{12,16},{16,20},{20,24},{24,28},{28,0},{1,5},{5... | collective-permute-start | bytes 589832 | tf_op jit(solution)/shard_map/while/body/eval_jaxpr/ppermute | solution.py:34
  439.9 21.6 %collective-permute-start = (bf16[2,256,3,64]{1,3,2,0:T(8,128)(2,1)S(1)}, bf16[2,256,3,64]{1,3,2,0:T(8,128)(2,1)}, u32[]{:S(2)}, u32[]{:S(2)}) collective-permute-start(bf16[2,256,3,64]{1,3,2,0:T(8,128)(2,1)S(1)} %copy.63), channel_id=1, source_target_pairs={{0,4},{4,8},{8,12},{12,16},{16,20},{20,24},{24,28},{28,0},{1,5},{5... | collective-permute-start | bytes 589832 | tf_op jit(solution)/shard_map/while/body/eval_jaxpr/ppermute | solution.py:34
  440.9 20.7 %collective-permute-start.1 = (bf16[2,256,3,64]{1,3,2,0:T(8,128)(2,1)S(1)}, bf16[2,256,3,64]{1,3,2,0:T(8,128)(2,1)}, u32[]{:S(2)}, u32[]{:S(2)}) collective-permute-start(bf16[2,256,3,64]{1,3,2,0:T(8,128)(2,1)S(1)} %copy.64), channel_id=1, source_target_pairs={{0,4},{4,8},{8,12},{12,16},{16,20},{20,24},{24,28},{28,0},{1,5},{5... | collective-permute-start | bytes 589832 | tf_op jit(solution)/shard_map/while/body/eval_jaxpr/ppermute | solution.py:34
  443.9 14.8 %collective-permute-start.2 = (bf16[2,256,3,64]{1,3,2,0:T(8,128)(2,1)}, bf16[2,256,3,64]{1,3,2,0:T(8,128)(2,1)}, u32[]{:S(2)}, u32[]{:S(2)}) collective-permute-start(bf16[2,256,3,64]{1,3,2,0:T(8,128)(2,1)} %fusion.105), channel_id=1, source_target_pairs={{0,4},{4,8},{8,12},{12,16},{16,20},{20,24},{24,28},{28,0},{1,5},{5... | collective-permute-start | bytes 589832 | tf_op jit(solution)/shard_map/while/body/eval_jaxpr/ppermute | solution.py:34
  446.0 14.7 %collective-permute-start.3 = (bf16[2,256,3,64]{1,3,2,0:T(8,128)(2,1)}, bf16[2,256,3,64]{1,3,2,0:T(8,128)(2,1)S(1)}, u32[]{:S(2)}, u32[]{:S(2)}) collective-permute-start(bf16[2,256,3,64]{1,3,2,0:T(8,128)(2,1)} %fusion.106), channel_id=1, source_target_pairs={{0,4},{4,8},{8,12},{12,16},{16,20},{20,24},{24,28},{28,0},{1,5},{5... | collective-permute-start | bytes 589832 | tf_op jit(solution)/shard_map/while/body/eval_jaxpr/ppermute | solution.py:34
  462.5 19.0 %collective-permute-start = (bf16[2,256,3,64]{1,3,2,0:T(8,128)(2,1)S(1)}, bf16[2,256,3,64]{1,3,2,0:T(8,128)(2,1)}, u32[]{:S(2)}, u32[]{:S(2)}) collective-permute-start(bf16[2,256,3,64]{1,3,2,0:T(8,128)(2,1)S(1)} %copy.63), channel_id=1, source_target_pairs={{0,4},{4,8},{8,12},{12,16},{16,20},{20,24},{24,28},{28,0},{1,5},{5... | collective-permute-start | bytes 589832 | tf_op jit(solution)/shard_map/while/body/eval_jaxpr/ppermute | solution.py:34
  463.4 18.1 %collective-permute-start.1 = (bf16[2,256,3,64]{1,3,2,0:T(8,128)(2,1)S(1)}, bf16[2,256,3,64]{1,3,2,0:T(8,128)(2,1)}, u32[]{:S(2)}, u32[]{:S(2)}) collective-permute-start(bf16[2,256,3,64]{1,3,2,0:T(8,128)(2,1)S(1)} %copy.64), channel_id=1, source_target_pairs={{0,4},{4,8},{8,12},{12,16},{16,20},{20,24},{24,28},{28,0},{1,5},{5... | collective-permute-start | bytes 589832 | tf_op jit(solution)/shard_map/while/body/eval_jaxpr/ppermute | solution.py:34
  466.5 12.2 %collective-permute-start.2 = (bf16[2,256,3,64]{1,3,2,0:T(8,128)(2,1)}, bf16[2,256,3,64]{1,3,2,0:T(8,128)(2,1)}, u32[]{:S(2)}, u32[]{:S(2)}) collective-permute-start(bf16[2,256,3,64]{1,3,2,0:T(8,128)(2,1)} %fusion.105), channel_id=1, source_target_pairs={{0,4},{4,8},{8,12},{12,16},{16,20},{20,24},{24,28},{28,0},{1,5},{5... | collective-permute-start | bytes 589832 | tf_op jit(solution)/shard_map/while/body/eval_jaxpr/ppermute | solution.py:34
  468.5 12.1 %collective-permute-start.3 = (bf16[2,256,3,64]{1,3,2,0:T(8,128)(2,1)}, bf16[2,256,3,64]{1,3,2,0:T(8,128)(2,1)S(1)}, u32[]{:S(2)}, u32[]{:S(2)}) collective-permute-start(bf16[2,256,3,64]{1,3,2,0:T(8,128)(2,1)} %fusion.106), channel_id=1, source_target_pairs={{0,4},{4,8},{8,12},{12,16},{16,20},{20,24},{24,28},{28,0},{1,5},{5... | collective-permute-start | bytes 589832 | tf_op jit(solution)/shard_map/while/body/eval_jaxpr/ppermute | solution.py:34
  482.4 18.3 %collective-permute-start = (bf16[2,256,3,64]{1,3,2,0:T(8,128)(2,1)S(1)}, bf16[2,256,3,64]{1,3,2,0:T(8,128)(2,1)}, u32[]{:S(2)}, u32[]{:S(2)}) collective-permute-start(bf16[2,256,3,64]{1,3,2,0:T(8,128)(2,1)S(1)} %copy.63), channel_id=1, source_target_pairs={{0,4},{4,8},{8,12},{12,16},{16,20},{20,24},{24,28},{28,0},{1,5},{5... | collective-permute-start | bytes 589832 | tf_op jit(solution)/shard_map/while/body/eval_jaxpr/ppermute | solution.py:34
  483.3 17.4 %collective-permute-start.1 = (bf16[2,256,3,64]{1,3,2,0:T(8,128)(2,1)S(1)}, bf16[2,256,3,64]{1,3,2,0:T(8,128)(2,1)}, u32[]{:S(2)}, u32[]{:S(2)}) collective-permute-start(bf16[2,256,3,64]{1,3,2,0:T(8,128)(2,1)S(1)} %copy.64), channel_id=1, source_target_pairs={{0,4},{4,8},{8,12},{12,16},{16,20},{20,24},{24,28},{28,0},{1,5},{5... | collective-permute-start | bytes 589832 | tf_op jit(solution)/shard_map/while/body/eval_jaxpr/ppermute | solution.py:34
  486.4 11.5 %collective-permute-start.2 = (bf16[2,256,3,64]{1,3,2,0:T(8,128)(2,1)}, bf16[2,256,3,64]{1,3,2,0:T(8,128)(2,1)}, u32[]{:S(2)}, u32[]{:S(2)}) collective-permute-start(bf16[2,256,3,64]{1,3,2,0:T(8,128)(2,1)} %fusion.105), channel_id=1, source_target_pairs={{0,4},{4,8},{8,12},{12,16},{16,20},{20,24},{24,28},{28,0},{1,5},{5... | collective-permute-start | bytes 589832 | tf_op jit(solution)/shard_map/while/body/eval_jaxpr/ppermute | solution.py:34
  488.5 11.4 %collective-permute-start.3 = (bf16[2,256,3,64]{1,3,2,0:T(8,128)(2,1)}, bf16[2,256,3,64]{1,3,2,0:T(8,128)(2,1)S(1)}, u32[]{:S(2)}, u32[]{:S(2)}) collective-permute-start(bf16[2,256,3,64]{1,3,2,0:T(8,128)(2,1)} %fusion.106), channel_id=1, source_target_pairs={{0,4},{4,8},{8,12},{12,16},{16,20},{20,24},{24,28},{28,0},{1,5},{5... | collective-permute-start | bytes 589832 | tf_op jit(solution)/shard_map/while/body/eval_jaxpr/ppermute | solution.py:34
  501.6 18.3 %collective-permute-start = (bf16[2,256,3,64]{1,3,2,0:T(8,128)(2,1)S(1)}, bf16[2,256,3,64]{1,3,2,0:T(8,128)(2,1)}, u32[]{:S(2)}, u32[]{:S(2)}) collective-permute-start(bf16[2,256,3,64]{1,3,2,0:T(8,128)(2,1)S(1)} %copy.63), channel_id=1, source_target_pairs={{0,4},{4,8},{8,12},{12,16},{16,20},{20,24},{24,28},{28,0},{1,5},{5... | collective-permute-start | bytes 589832 | tf_op jit(solution)/shard_map/while/body/eval_jaxpr/ppermute | solution.py:34
  502.6 17.4 %collective-permute-start.1 = (bf16[2,256,3,64]{1,3,2,0:T(8,128)(2,1)S(1)}, bf16[2,256,3,64]{1,3,2,0:T(8,128)(2,1)}, u32[]{:S(2)}, u32[]{:S(2)}) collective-permute-start(bf16[2,256,3,64]{1,3,2,0:T(8,128)(2,1)S(1)} %copy.64), channel_id=1, source_target_pairs={{0,4},{4,8},{8,12},{12,16},{16,20},{20,24},{24,28},{28,0},{1,5},{5... | collective-permute-start | bytes 589832 | tf_op jit(solution)/shard_map/while/body/eval_jaxpr/ppermute | solution.py:34
  508.4 8.7 %collective-permute-start.2 = (bf16[2,256,3,64]{1,3,2,0:T(8,128)(2,1)}, bf16[2,256,3,64]{1,3,2,0:T(8,128)(2,1)}, u32[]{:S(2)}, u32[]{:S(2)}) collective-permute-start(bf16[2,256,3,64]{1,3,2,0:T(8,128)(2,1)} %fusion.105), channel_id=1, source_target_pairs={{0,4},{4,8},{8,12},{12,16},{16,20},{20,24},{24,28},{28,0},{1,5},{5... | collective-permute-start | bytes 589832 | tf_op jit(solution)/shard_map/while/body/eval_jaxpr/ppermute | solution.py:34
  510.4 8.7 %collective-permute-start.3 = (bf16[2,256,3,64]{1,3,2,0:T(8,128)(2,1)}, bf16[2,256,3,64]{1,3,2,0:T(8,128)(2,1)S(1)}, u32[]{:S(2)}, u32[]{:S(2)}) collective-permute-start(bf16[2,256,3,64]{1,3,2,0:T(8,128)(2,1)} %fusion.106), channel_id=1, source_target_pairs={{0,4},{4,8},{8,12},{12,16},{16,20},{20,24},{24,28},{28,0},{1,5},{5... | collective-permute-start | bytes 589832 | tf_op jit(solution)/shard_map/while/body/eval_jaxpr/ppermute | solution.py:34
  520.9 25.4 %collective-permute-start = (bf16[2,256,3,64]{1,3,2,0:T(8,128)(2,1)S(1)}, bf16[2,256,3,64]{1,3,2,0:T(8,128)(2,1)}, u32[]{:S(2)}, u32[]{:S(2)}) collective-permute-start(bf16[2,256,3,64]{1,3,2,0:T(8,128)(2,1)S(1)} %copy.63), channel_id=1, source_target_pairs={{0,4},{4,8},{8,12},{12,16},{16,20},{20,24},{24,28},{28,0},{1,5},{5... | collective-permute-start | bytes 589832 | tf_op jit(solution)/shard_map/while/body/eval_jaxpr/ppermute | solution.py:34
  521.8 24.5 %collective-permute-start.1 = (bf16[2,256,3,64]{1,3,2,0:T(8,128)(2,1)S(1)}, bf16[2,256,3,64]{1,3,2,0:T(8,128)(2,1)}, u32[]{:S(2)}, u32[]{:S(2)}) collective-permute-start(bf16[2,256,3,64]{1,3,2,0:T(8,128)(2,1)S(1)} %copy.64), channel_id=1, source_target_pairs={{0,4},{4,8},{8,12},{12,16},{16,20},{20,24},{24,28},{28,0},{1,5},{5... | collective-permute-start | bytes 589832 | tf_op jit(solution)/shard_map/while/body/eval_jaxpr/ppermute | solution.py:34
  525.8 17.6 %collective-permute-start.2 = (bf16[2,256,3,64]{1,3,2,0:T(8,128)(2,1)}, bf16[2,256,3,64]{1,3,2,0:T(8,128)(2,1)}, u32[]{:S(2)}, u32[]{:S(2)}) collective-permute-start(bf16[2,256,3,64]{1,3,2,0:T(8,128)(2,1)} %fusion.105), channel_id=1, source_target_pairs={{0,4},{4,8},{8,12},{12,16},{16,20},{20,24},{24,28},{28,0},{1,5},{5... | collective-permute-start | bytes 589832 | tf_op jit(solution)/shard_map/while/body/eval_jaxpr/ppermute | solution.py:34
  528.4 17.1 %collective-permute-start.3 = (bf16[2,256,3,64]{1,3,2,0:T(8,128)(2,1)}, bf16[2,256,3,64]{1,3,2,0:T(8,128)(2,1)S(1)}, u32[]{:S(2)}, u32[]{:S(2)}) collective-permute-start(bf16[2,256,3,64]{1,3,2,0:T(8,128)(2,1)} %fusion.106), channel_id=1, source_target_pairs={{0,4},{4,8},{8,12},{12,16},{16,20},{20,24},{24,28},{28,0},{1,5},{5... | collective-permute-start | bytes 589832 | tf_op jit(solution)/shard_map/while/body/eval_jaxpr/ppermute | solution.py:34
  549.7 7.4 copy-start.21
  549.7 7.4 copy-start.30
  549.7 7.4 copy-start.36
  551.7 17.1 %all-to-all-start.3 = ((bf16[2,256,3,1,192]{4,0,3,2,1:T(2,128)(2,1)}), bf16[2,256,3,1,192]{4,0,3,2,1:T(2,128)(2,1)S(1)}, u32[]{:S(2)}, u32[]{:S(2)}) async-start(bf16[2,256,3,1,192]{4,0,3,2,1:T(2,128)(2,1)} %copy.48), calls=%async_computation.3 | async-start | bytes 1572864 | tf_op jit(solution)/shard_map/all_to_all | solution.py:228
  557.1 278.4 %reduce-scatter.7.cloned.1.call-start = ((), (), s32[]{:S(2)}) async-start(), calls=%async_computation.13 | async-start | bytes 7299072 | tf_op jit(solution)/shard_map/reduce_scatter | solution.py:238
  577.1 41.6 %copy-start.6 = (f32[128,768]{1,0:T(8,128)S(1)}, f32[128,768]{1,0:T(8,128)}, u32[]{:S(2)}) copy-start(f32[128,768]{1,0:T(8,128)} %copy-done.5) | copy-start | bytes 1179652
  (49 other events, 120.3 us)
Sparse Core Ops, SparseCore 0:
  10.9 62.8 all-gather.5
  96.7 63.0 all-gather.7
  162.6 53.6 all-gather.9
  219.1 59.0 all-gather.11
  280.9 54.4 all-gather.13
  343.1 114.0 reduce-scatter.8
  464.1 121.4 reduce-scatter.12
  592.8 118.0 reduce-scatter.10
  717.1 118.3 reduce-scatter.6
